TPU v7x, 256 devices: a whole 4x4x8 slice. The times are simulated.
256 devices in a mesh: row: 32 (over y_lo, z, core), col: 8 (over y_hi, x).
Axes of the slice: x: 4, y: 4 (y_hi: 2, y_lo: 2; y = y_hi * 2 + y_lo), z: 8, core: 2. Of those that a mesh axis runs over, the one named last changes fastest.
Arguments:
- alignment: bfloat16 [128, 1536, 256], P('row', 'col'), may hold values from -10 to 10
- alignment_norm_gain: float32 [256], replicated, may hold values from 0.1 to 1.9
- alignment_norm_bias: float32 [256], replicated, may hold values from -1.75 to 1.75
- projection_weight: bfloat16 [256, 64], replicated, may hold values from -0.375 to 0.375
- projection_bias_pair: float32 [64], replicated, may hold values from -3 to 3
- w_out: bfloat16 [1024, 128], replicated, may hold values from -0.1875 to 0.1875
- b_out: float32 [128], replicated, may hold values from -1.75 to 1.75
- pair_gain: float32 [128], replicated, may hold values from 0.1 to 1.9
- pair_bias: float32 [128], replicated, may hold values from -1.75 to 1.75
- w_up: bfloat16 [128, 512], replicated, may hold values from -0.5 to 0.5
- b_up: float32 [512], replicated, may hold values from -1.75 to 1.75
- w_down: bfloat16 [512, 128], replicated, may hold values from -0.25 to 0.25
- b_down: float32 [128], replicated, may hold values from -1.75 to 1.75
Outputs:
- pair_out: bfloat16 [1536, 1536, 128], P('row', 'col')
All inputs are finite; a program needn't handle non-finite values.
Results may differ from a plain program's by a relative error of at most 0.0052.
Values may be sent and summed in bfloat16 or wider, within the bound.
A program may use at most 64 MiB of HBM per device.

v0:
```python
import math

import jax
import jax.numpy as jnp
from jax import lax
from jax.sharding import PartitionSpec as P

EPSILON = 1e-05


def layer_norm(values, gain_vec, bias_vec):
    average = jnp.mean(values, axis=-1, keepdims=True)
    centered = values - average
    variance = jnp.mean(centered * centered, axis=-1, keepdims=True)
    return centered * lax.rsqrt(variance + EPSILON) * gain_vec + bias_vec


def channel_norm(values, gain_vec, bias_vec):
    average = jnp.mean(values, axis=0, keepdims=True)
    centered = values - average
    variance = jnp.mean(centered * centered, axis=0, keepdims=True)
    return (
        centered * lax.rsqrt(variance + EPSILON) * gain_vec[:, None, None] + bias_vec[:, None, None]
    )


def project_split(
    rows_in,
    seq_rows,
    residues,
    alignment_norm_gain,
    alignment_norm_bias,
    projection_weight,
    projection_bias_pair,
):
    channel_count = rows_in.shape[-1]
    width = projection_weight.shape[1]
    half_width = width // 2
    normed = layer_norm(
        rows_in.reshape(seq_rows * residues, channel_count).astype(jnp.float32),
        alignment_norm_gain,
        alignment_norm_bias,
    ).astype(jnp.bfloat16)
    result = (
        jnp.dot(normed, projection_weight, preferred_element_type=jnp.float32)
        + projection_bias_pair
    ).astype(jnp.bfloat16)
    return result.reshape(seq_rows, residues, 2, half_width).transpose(0, 2, 3, 1)


def outer_channels(rows_side, cols_side, weight, bias_vec, total):
    seq_rows, block_size, half_width = rows_side.shape
    column_length = cols_side.shape[2]
    flat_cols = cols_side.reshape(seq_rows, half_width * column_length)
    product = (
        lax.dot_general(
            rows_side, flat_cols, (((0,), (0,)), ((), ())), preferred_element_type=jnp.float32
        )
        / total
    )
    product = product.astype(jnp.bfloat16).reshape(
        block_size, half_width * half_width, column_length
    )
    projected_z = lax.dot_general(
        weight, product, (((0,), (1,)), ((), ())), preferred_element_type=jnp.float32
    )
    return jax.nn.relu(projected_z + bias_vec[:, None, None])


def finish(pair, pair_gain, pair_bias, w_up, b_up, w_down, b_down):
    normed = channel_norm(pair, pair_gain, pair_bias).astype(jnp.bfloat16)
    hidden = lax.dot_general(
        w_up, normed, (((0,), (0,)), ((), ())), preferred_element_type=jnp.float32
    )
    hidden = jax.nn.relu(hidden + b_up[:, None, None]).astype(jnp.bfloat16)
    update = lax.dot_general(
        w_down, hidden, (((0,), (0,)), ((), ())), preferred_element_type=jnp.float32
    )
    result = (pair + update + b_down[:, None, None]).astype(jnp.bfloat16)
    return result.transpose(1, 2, 0)


def shards(
    alignment,
    alignment_norm_gain,
    alignment_norm_bias,
    projection_weight,
    projection_bias_pair,
    w_out,
    b_out,
    pair_gain,
    pair_bias,
    w_up,
    b_up,
    w_down,
    b_down,
):
    alignment_local, column_length, channel_count = alignment.shape
    projection_width = projection_weight.shape[1]
    half_width = projection_width // 2
    row_count = lax.axis_size("row")
    col_count = lax.axis_size("col")
    row_length = column_length * col_count // row_count
    local_projected = project_split(
        alignment,
        alignment_local,
        column_length,
        alignment_norm_gain,
        alignment_norm_bias,
        projection_weight,
        projection_bias_pair,
    )
    column_projected = lax.all_gather(local_projected, "row", axis=0, tiled=True)
    alignment_total = column_projected.shape[0]
    col_wide = lax.all_gather(local_projected, "col", axis=3, tiled=True)
    row_projected = lax.all_to_all(col_wide, "row", split_axis=3, concat_axis=0, tiled=True)
    col_left = column_projected[:, 0]
    col_right = column_projected[:, 1]
    row_left = row_projected[:, 0]
    row_right = row_projected[:, 1]
    out_width = w_out.shape[1]
    w_mirror = (
        w_out.reshape(half_width, half_width, out_width)
        .transpose(1, 0, 2)
        .reshape(half_width * half_width, out_width)
    )
    block_size = math.gcd(row_length, 8)

    def pair_block(block_index):
        first_row = block_index * block_size
        left_here = lax.dynamic_slice_in_dim(row_left, first_row, block_size, 2).transpose(0, 2, 1)
        right_here = lax.dynamic_slice_in_dim(row_right, first_row, block_size, 2).transpose(
            0, 2, 1
        )
        pair = outer_channels(left_here, col_right, w_out, b_out, alignment_total)
        pair = pair + outer_channels(right_here, col_left, w_mirror, b_out, alignment_total)
        return finish(pair, pair_gain, pair_bias, w_up, b_up, w_down, b_down)

    blocks_out = lax.map(pair_block, jnp.arange(row_length // block_size, dtype=jnp.int32))
    return blocks_out.reshape(row_length, column_length, out_width)


def solution(mesh):
    return jax.shard_map(
        shards,
        mesh=mesh,
        in_specs=(
            P("row", "col", None),
            P(),
            P(),
            P(),
            P(),
            P(),
            P(),
            P(),
            P(),
            P(),
            P(),
            P(),
            P(),
        ),
        out_specs=P("row", "col", None),
        check_vma=False,
    )
```

profile of v0, /device:TPU:1, one launch (start us, length us, event | category | flops | bytes accessed | tf_op | source)
XLA Modules:
  0.0 304.4 jit_solution(11563125858991436969)
XLA Ops:
  13.4 40.8 %all_gather.6 = bf16[4,2,32,1536]{2,0,1,3:T(4,128)(2,1)S(1)} all-gather(bf16[4,2,32,192]{2,0,1,3:T(4,128)(2,1)} %bitcast.131), channel_id=1, replica_groups=mesh['row'=32,'col'=8] {'col'}, dimensions={3}, use_global_device_ids=true | all-gather | bytes 884736 | tf_op jit(solution)/shard_map/all_gather | solution.py:115
  54.2 3.7 %reshape.86 = bf16[32,2,6144]{2,1,0:T(2,128)(2,1)} reshape(bf16[1536,2,4,32]{3,2,1,0:T(4,128)(2,1)S(1)} %bitcast.126) | data formatting | bytes 1572864
  57.9 14.1 %all-to-all-start = ((bf16[32,2,6144]{2,1,0:T(2,128)(2,1)}), bf16[32,2,6144]{2,1,0:T(2,128)(2,1)}, u32[]{:S(2)}, u32[]{:S(2)}) async-start(bf16[32,2,6144]{2,1,0:T(2,128)(2,1)} %reshape.86), calls=%async_computation | async-start | bytes 1572864 | tf_op jit(solution)/shard_map/all_to_all | solution.py:116
  73.1 27.1 %all-to-all-done = bf16[32,2,6144]{2,1,0:T(2,128)(2,1)} async-done(((bf16[32,2,6144]{2,1,0:T(2,128)(2,1)}), bf16[32,2,6144]{2,1,0:T(2,128)(2,1)}, u32[]{:S(2)}, u32[]{:S(2)}) %all-to-all-start) | async-done | bytes 786464 | tf_op jit(solution)/shard_map/all_to_all | solution.py:116
  100.2 5.0 %reshape.87 = bf16[1536,2,4,32]{3,2,1,0:T(4,128)(2,1)S(1)} reshape(bf16[32,2,6144]{2,1,0:T(2,128)(2,1)} %all-to-all-done) | data formatting | bytes 1572864
  105.2 4.6 %copy.45 = bf16[4,2,32,32,48]{4,2,1,0,3:T(8,128)(2,1)} copy(bf16[4,2,32,32,48]{2,0,1,4,3:T(4,128)(2,1)S(1)} %bitcast.127) | data formatting | bytes 1572864 | tf_op jit(solution)/shard_map/all_to_all | solution.py:116
  109.7 1.9 slice_bitcast_fusion
  111.6 2.2 copy.48
  113.8 2.2 copy.50
  116.0 4.1 %fusion.47 = (bf16[128,1,32,192]{3,2,1,0:T(8,128)(2,1)S(1)}, bf16[128,1,32,192]{3,2,1,0:T(8,128)(2,1)}) fusion(bf16[128,2,32,192]{3,2,1,0:T(8,128)(2,1)} %all-gather.2.cloned.1.call-done), kind=kLoop, calls=%fused_computation.51 | loop fusion | bytes 6291456 | tf_op jit(solution)/shard_map/slice | solution.py:117
  120.0 4.5 %copy.49 = bf16[128,1,32,192]{0,3,2,1:T(8,128)(2,1)} copy(bf16[128,1,32,192]{3,2,1,0:T(8,128)(2,1)} %get-tuple-element.171) | data formatting | bytes 3145728 | tf_op jit(solution)/shard_map/while | solution.py:139
  124.5 2.9 copy.51
  127.5 170.1 %while.10 = (s32[]{:T(128)}, bf16[6,8,192,128]{3,2,1,0:T(8,128)(2,1)}, s32[6]{0:T(128)S(1)}, bf16[128,32,48]{0,1,2:T(8,128)(2,1)}, bf16[128,1,32,192]{0,3,2,1:T(...) while((s32[]{:T(128)}, ...), condition=%wide.region_5.6_spmd, body=%wide.region_2.5_spmd.sunk | while | flops 2025260544 | bytes 41745736 | solution.py:139
  128.9 2.4 fusion.78
  131.4 5.9 %reshape.90 = bf16[8,1024,192]{2,1,0:T(8,128)(2,1)} reshape(bf16[8,32,6144]{2,1,0:T(8,128)(2,1)S(1)} %fusion.78) | data formatting | bytes 6291456 | tf_op jit(solution)/shard_map/while/body/eval_jaxpr/reshape | solution.py:61
  137.3 4.5 %fusion.79 = f32[8,192,128]{2,1,0:T(8,128)} fusion(bf16[8,1024,192]{2,1,0:T(8,128)(2,1)} %reshape.90, f32[128]{0:T(128)S(1)} %get-tuple-element.321, bf16[1024,128]{1,0:T(8,128)(2,1)} %get-tuple-element.320), kind=kOutput, calls=%fused_computation.13.clone.1 | convolution fusion | flops 403046400 | bytes 4194816 | tf_op jit(solution)/shard_map/while/body/eval_jaxpr/dot_general | solution.py:64
  143.6 5.9 %reshape.91 = bf16[8,1024,192]{2,1,0:T(8,128)(2,1)} reshape(bf16[8,32,6144]{2,1,0:T(8,128)(2,1)S(1)} %fusion.80) | data formatting | bytes 6291456 | tf_op jit(solution)/shard_map/while/body/eval_jaxpr/reshape | solution.py:61
  149.5 4.0 %bitcast_reduce_fusion.2 = (f32[8,192]{1,0:T(8,128)S(1)}, f32[8,192,128]{2,1,0:T(8,128)S(1)}) fusion(f32[8,192,128]{2,1,0:T(8,128)} %fusion.79, f32[128]{0:T(128)S(1)} %get-tuple-element.321, bf16[8,1024,192]{2,1,0:T(8,128)(2,1)} %reshape.91, bf16[1024,128]{1,0:T(8,128)(2,1)S(1)} %get-tuple-element.324), kind=kOutput, calls=%fused_computation.18.clone.1 | convolution fusion | flops 403438080 | bytes 4987392 | tf_op jit(solution)/shard_map/while/body/eval_jaxpr/dot_general | solution.py:64
  157.3 2.4 fusion.78
  159.7 5.9 %reshape.90 = bf16[8,1024,192]{2,1,0:T(8,128)(2,1)} reshape(bf16[8,32,6144]{2,1,0:T(8,128)(2,1)S(1)} %fusion.78) | data formatting | bytes 6291456 | tf_op jit(solution)/shard_map/while/body/eval_jaxpr/reshape | solution.py:61
  165.6 4.5 %fusion.79 = f32[8,192,128]{2,1,0:T(8,128)} fusion(bf16[8,1024,192]{2,1,0:T(8,128)(2,1)} %reshape.90, f32[128]{0:T(128)S(1)} %get-tuple-element.321, bf16[1024,128]{1,0:T(8,128)(2,1)} %get-tuple-element.320), kind=kOutput, calls=%fused_computation.13.clone.1 | convolution fusion | flops 403046400 | bytes 4194816 | tf_op jit(solution)/shard_map/while/body/eval_jaxpr/dot_general | solution.py:64
  170.1 1.8 fusion.80
  171.9 5.9 %reshape.91 = bf16[8,1024,192]{2,1,0:T(8,128)(2,1)} reshape(bf16[8,32,6144]{2,1,0:T(8,128)(2,1)S(1)} %fusion.80) | data formatting | bytes 6291456 | tf_op jit(solution)/shard_map/while/body/eval_jaxpr/reshape | solution.py:61
  177.8 4.0 %bitcast_reduce_fusion.2 = (f32[8,192]{1,0:T(8,128)S(1)}, f32[8,192,128]{2,1,0:T(8,128)S(1)}) fusion(f32[8,192,128]{2,1,0:T(8,128)} %fusion.79, f32[128]{0:T(128)S(1)} %get-tuple-element.321, bf16[8,1024,192]{2,1,0:T(8,128)(2,1)} %reshape.91, bf16[1024,128]{1,0:T(8,128)(2,1)S(1)} %get-tuple-element.324), kind=kOutput, calls=%fused_computation.18.clone.1 | convolution fusion | flops 403438080 | bytes 4987392 | tf_op jit(solution)/shard_map/while/body/eval_jaxpr/dot_general | solution.py:64
  185.6 2.4 fusion.78
  188.0 5.9 %reshape.90 = bf16[8,1024,192]{2,1,0:T(8,128)(2,1)} reshape(bf16[8,32,6144]{2,1,0:T(8,128)(2,1)S(1)} %fusion.78) | data formatting | bytes 6291456 | tf_op jit(solution)/shard_map/while/body/eval_jaxpr/reshape | solution.py:61
  193.9 4.5 %fusion.79 = f32[8,192,128]{2,1,0:T(8,128)} fusion(bf16[8,1024,192]{2,1,0:T(8,128)(2,1)} %reshape.90, f32[128]{0:T(128)S(1)} %get-tuple-element.321, bf16[1024,128]{1,0:T(8,128)(2,1)} %get-tuple-element.320), kind=kOutput, calls=%fused_computation.13.clone.1 | convolution fusion | flops 403046400 | bytes 4194816 | tf_op jit(solution)/shard_map/while/body/eval_jaxpr/dot_general | solution.py:64
  198.4 1.8 fusion.80
  200.2 5.9 %reshape.91 = bf16[8,1024,192]{2,1,0:T(8,128)(2,1)} reshape(bf16[8,32,6144]{2,1,0:T(8,128)(2,1)S(1)} %fusion.80) | data formatting | bytes 6291456 | tf_op jit(solution)/shard_map/while/body/eval_jaxpr/reshape | solution.py:61
  206.1 4.0 %bitcast_reduce_fusion.2 = (f32[8,192]{1,0:T(8,128)S(1)}, f32[8,192,128]{2,1,0:T(8,128)S(1)}) fusion(f32[8,192,128]{2,1,0:T(8,128)} %fusion.79, f32[128]{0:T(128)S(1)} %get-tuple-element.321, bf16[8,1024,192]{2,1,0:T(8,128)(2,1)} %reshape.91, bf16[1024,128]{1,0:T(8,128)(2,1)S(1)} %get-tuple-element.324), kind=kOutput, calls=%fused_computation.18.clone.1 | convolution fusion | flops 403438080 | bytes 4987392 | tf_op jit(solution)/shard_map/while/body/eval_jaxpr/dot_general | solution.py:64
  213.9 2.4 fusion.78
  216.3 5.9 %reshape.90 = bf16[8,1024,192]{2,1,0:T(8,128)(2,1)} reshape(bf16[8,32,6144]{2,1,0:T(8,128)(2,1)S(1)} %fusion.78) | data formatting | bytes 6291456 | tf_op jit(solution)/shard_map/while/body/eval_jaxpr/reshape | solution.py:61
  222.2 4.5 %fusion.79 = f32[8,192,128]{2,1,0:T(8,128)} fusion(bf16[8,1024,192]{2,1,0:T(8,128)(2,1)} %reshape.90, f32[128]{0:T(128)S(1)} %get-tuple-element.321, bf16[1024,128]{1,0:T(8,128)(2,1)} %get-tuple-element.320), kind=kOutput, calls=%fused_computation.13.clone.1 | convolution fusion | flops 403046400 | bytes 4194816 | tf_op jit(solution)/shard_map/while/body/eval_jaxpr/dot_general | solution.py:64
  226.7 1.8 fusion.80
  228.6 5.9 %reshape.91 = bf16[8,1024,192]{2,1,0:T(8,128)(2,1)} reshape(bf16[8,32,6144]{2,1,0:T(8,128)(2,1)S(1)} %fusion.80) | data formatting | bytes 6291456 | tf_op jit(solution)/shard_map/while/body/eval_jaxpr/reshape | solution.py:61
  234.5 4.0 %bitcast_reduce_fusion.2 = (f32[8,192]{1,0:T(8,128)S(1)}, f32[8,192,128]{2,1,0:T(8,128)S(1)}) fusion(f32[8,192,128]{2,1,0:T(8,128)} %fusion.79, f32[128]{0:T(128)S(1)} %get-tuple-element.321, bf16[8,1024,192]{2,1,0:T(8,128)(2,1)} %reshape.91, bf16[1024,128]{1,0:T(8,128)(2,1)S(1)} %get-tuple-element.324), kind=kOutput, calls=%fused_computation.18.clone.1 | convolution fusion | flops 403438080 | bytes 4987392 | tf_op jit(solution)/shard_map/while/body/eval_jaxpr/dot_general | solution.py:64
  242.2 2.4 fusion.78
  244.6 5.9 %reshape.90 = bf16[8,1024,192]{2,1,0:T(8,128)(2,1)} reshape(bf16[8,32,6144]{2,1,0:T(8,128)(2,1)S(1)} %fusion.78) | data formatting | bytes 6291456 | tf_op jit(solution)/shard_map/while/body/eval_jaxpr/reshape | solution.py:61
  250.5 4.5 %fusion.79 = f32[8,192,128]{2,1,0:T(8,128)} fusion(bf16[8,1024,192]{2,1,0:T(8,128)(2,1)} %reshape.90, f32[128]{0:T(128)S(1)} %get-tuple-element.321, bf16[1024,128]{1,0:T(8,128)(2,1)} %get-tuple-element.320), kind=kOutput, calls=%fused_computation.13.clone.1 | convolution fusion | flops 403046400 | bytes 4194816 | tf_op jit(solution)/shard_map/while/body/eval_jaxpr/dot_general | solution.py:64
  255.0 1.8 fusion.80
  256.9 5.9 %reshape.91 = bf16[8,1024,192]{2,1,0:T(8,128)(2,1)} reshape(bf16[8,32,6144]{2,1,0:T(8,128)(2,1)S(1)} %fusion.80) | data formatting | bytes 6291456 | tf_op jit(solution)/shard_map/while/body/eval_jaxpr/reshape | solution.py:61
  262.8 4.0 %bitcast_reduce_fusion.2 = (f32[8,192]{1,0:T(8,128)S(1)}, f32[8,192,128]{2,1,0:T(8,128)S(1)}) fusion(f32[8,192,128]{2,1,0:T(8,128)} %fusion.79, f32[128]{0:T(128)S(1)} %get-tuple-element.321, bf16[8,1024,192]{2,1,0:T(8,128)(2,1)} %reshape.91, bf16[1024,128]{1,0:T(8,128)(2,1)S(1)} %get-tuple-element.324), kind=kOutput, calls=%fused_computation.18.clone.1 | convolution fusion | flops 403438080 | bytes 4987392 | tf_op jit(solution)/shard_map/while/body/eval_jaxpr/dot_general | solution.py:64
  270.5 2.4 fusion.78
  272.9 5.9 %reshape.90 = bf16[8,1024,192]{2,1,0:T(8,128)(2,1)} reshape(bf16[8,32,6144]{2,1,0:T(8,128)(2,1)S(1)} %fusion.78) | data formatting | bytes 6291456 | tf_op jit(solution)/shard_map/while/body/eval_jaxpr/reshape | solution.py:61
  278.8 4.5 %fusion.79 = f32[8,192,128]{2,1,0:T(8,128)} fusion(bf16[8,1024,192]{2,1,0:T(8,128)(2,1)} %reshape.90, f32[128]{0:T(128)S(1)} %get-tuple-element.321, bf16[1024,128]{1,0:T(8,128)(2,1)} %get-tuple-element.320), kind=kOutput, calls=%fused_computation.13.clone.1 | convolution fusion | flops 403046400 | bytes 4194816 | tf_op jit(solution)/shard_map/while/body/eval_jaxpr/dot_general | solution.py:64
  283.3 1.8 fusion.80
  285.2 5.9 %reshape.91 = bf16[8,1024,192]{2,1,0:T(8,128)(2,1)} reshape(bf16[8,32,6144]{2,1,0:T(8,128)(2,1)S(1)} %fusion.80) | data formatting | bytes 6291456 | tf_op jit(solution)/shard_map/while/body/eval_jaxpr/reshape | solution.py:61
  291.1 4.0 %bitcast_reduce_fusion.2 = (f32[8,192]{1,0:T(8,128)S(1)}, f32[8,192,128]{2,1,0:T(8,128)S(1)}) fusion(f32[8,192,128]{2,1,0:T(8,128)} %fusion.79, f32[128]{0:T(128)S(1)} %get-tuple-element.321, bf16[8,1024,192]{2,1,0:T(8,128)(2,1)} %reshape.91, bf16[1024,128]{1,0:T(8,128)(2,1)S(1)} %get-tuple-element.324), kind=kOutput, calls=%fused_computation.18.clone.1 | convolution fusion | flops 403438080 | bytes 4987392 | tf_op jit(solution)/shard_map/while/body/eval_jaxpr/dot_general | solution.py:64
  (96 shorter events, 28.1 us)
Async XLA Ops:
  6.5 4.1 %copy-start = (bf16[256,64]{0,1:T(8,128)(2,1)S(1)}, bf16[256,64]{0,1:T(8,128)(2,1)}, u32[]{:S(2)}) copy-start(bf16[256,64]{0,1:T(8,128)(2,1)} %param.18) | copy-start | bytes 98308
  6.5 109.4 %all-gather.2.cloned.1.call-start = ((), (), s32[]{:S(2)}) async-start(), calls=%async_computation.1 | async-start | bytes 4325376 | tf_op jit(solution)/shard_map/all_gather | solution.py:113
  57.9 42.3 %all-to-all-start = ((bf16[32,2,6144]{2,1,0:T(2,128)(2,1)}), bf16[32,2,6144]{2,1,0:T(2,128)(2,1)}, u32[]{:S(2)}, u32[]{:S(2)}) async-start(bf16[32,2,6144]{2,1,0:T(2,128)(2,1)} %reshape.86), calls=%async_computation | async-start | bytes 1572864 | tf_op jit(solution)/shard_map/all_to_all | solution.py:116
  120.0 7.4 %copy-start.2 = (f32[128]{0:T(128)S(1)}, f32[128]{0:T(128)}, u32[]{:S(2)}) copy-start(f32[128]{0:T(128)} %param.21) | copy-start | bytes 1540
  120.0 7.4 %copy-start.5 = (f32[512]{0:T(512)S(1)}, f32[512]{0:T(512)}, u32[]{:S(2)}) copy-start(f32[512]{0:T(512)} %param.25) | copy-start | bytes 6148
  120.0 7.4 %copy-start.6 = (f32[128]{0:T(128)S(1)}, f32[128]{0:T(128)}, u32[]{:S(2)}) copy-start(f32[128]{0:T(128)} %param.22) | copy-start | bytes 1540
  120.0 7.4 %copy-start.7 = (f32[128]{0:T(128)S(1)}, f32[128]{0:T(128)}, u32[]{:S(2)}) copy-start(f32[128]{0:T(128)} %param.23) | copy-start | bytes 1540
  120.0 7.4 %copy-start.8 = (f32[128]{0:T(128)S(1)}, f32[128]{0:T(128)}, u32[]{:S(2)}) copy-start(f32[128]{0:T(128)} %param.27) | copy-start | bytes 1540
  137.3 4.5 %copy-start.1 = (bf16[128,1,32,192]{0,3,2,1:T(8,128)(2,1)S(1)}, bf16[128,1,32,192]{0,3,2,1:T(8,128)(2,1)}, u32[]{:S(2)}) copy-start(bf16[128,1,32,192]{0,3,2,1:T(8,128)(2,1)} %get-tuple-element.323) | copy-start | bytes 4718596 | tf_op jit(solution)/shard_map/while
  149.5 4.6 %copy-start.3 = (bf16[128,512]{1,0:T(8,128)(2,1)S(1)}, bf16[128,512]{1,0:T(8,128)(2,1)}, u32[]{:S(2)}) copy-start(bf16[128,512]{1,0:T(8,128)(2,1)} %get-tuple-element.327) | copy-start | bytes 393220 | tf_op jit(solution)/shard_map/while
  149.5 4.6 %copy-start.4 = (bf16[512,128]{1,0:T(8,128)(2,1)S(1)}, bf16[512,128]{1,0:T(8,128)(2,1)}, u32[]{:S(2)}) copy-start(bf16[512,128]{1,0:T(8,128)(2,1)} %get-tuple-element.329) | copy-start | bytes 393220 | tf_op jit(solution)/shard_map/while
  165.6 4.5 %copy-start.1 = (bf16[128,1,32,192]{0,3,2,1:T(8,128)(2,1)S(1)}, bf16[128,1,32,192]{0,3,2,1:T(8,128)(2,1)}, u32[]{:S(2)}) copy-start(bf16[128,1,32,192]{0,3,2,1:T(8,128)(2,1)} %get-tuple-element.323) | copy-start | bytes 4718596 | tf_op jit(solution)/shard_map/while
  177.8 4.6 %copy-start.3 = (bf16[128,512]{1,0:T(8,128)(2,1)S(1)}, bf16[128,512]{1,0:T(8,128)(2,1)}, u32[]{:S(2)}) copy-start(bf16[128,512]{1,0:T(8,128)(2,1)} %get-tuple-element.327) | copy-start | bytes 393220 | tf_op jit(solution)/shard_map/while
  177.8 4.6 %copy-start.4 = (bf16[512,128]{1,0:T(8,128)(2,1)S(1)}, bf16[512,128]{1,0:T(8,128)(2,1)}, u32[]{:S(2)}) copy-start(bf16[512,128]{1,0:T(8,128)(2,1)} %get-tuple-element.329) | copy-start | bytes 393220 | tf_op jit(solution)/shard_map/while
  193.9 4.5 %copy-start.1 = (bf16[128,1,32,192]{0,3,2,1:T(8,128)(2,1)S(1)}, bf16[128,1,32,192]{0,3,2,1:T(8,128)(2,1)}, u32[]{:S(2)}) copy-start(bf16[128,1,32,192]{0,3,2,1:T(8,128)(2,1)} %get-tuple-element.323) | copy-start | bytes 4718596 | tf_op jit(solution)/shard_map/while
  206.1 4.6 %copy-start.3 = (bf16[128,512]{1,0:T(8,128)(2,1)S(1)}, bf16[128,512]{1,0:T(8,128)(2,1)}, u32[]{:S(2)}) copy-start(bf16[128,512]{1,0:T(8,128)(2,1)} %get-tuple-element.327) | copy-start | bytes 393220 | tf_op jit(solution)/shard_map/while
  206.1 4.6 %copy-start.4 = (bf16[512,128]{1,0:T(8,128)(2,1)S(1)}, bf16[512,128]{1,0:T(8,128)(2,1)}, u32[]{:S(2)}) copy-start(bf16[512,128]{1,0:T(8,128)(2,1)} %get-tuple-element.329) | copy-start | bytes 393220 | tf_op jit(solution)/shard_map/while
  222.2 4.5 %copy-start.1 = (bf16[128,1,32,192]{0,3,2,1:T(8,128)(2,1)S(1)}, bf16[128,1,32,192]{0,3,2,1:T(8,128)(2,1)}, u32[]{:S(2)}) copy-start(bf16[128,1,32,192]{0,3,2,1:T(8,128)(2,1)} %get-tuple-element.323) | copy-start | bytes 4718596 | tf_op jit(solution)/shard_map/while
  234.5 4.6 %copy-start.3 = (bf16[128,512]{1,0:T(8,128)(2,1)S(1)}, bf16[128,512]{1,0:T(8,128)(2,1)}, u32[]{:S(2)}) copy-start(bf16[128,512]{1,0:T(8,128)(2,1)} %get-tuple-element.327) | copy-start | bytes 393220 | tf_op jit(solution)/shard_map/while
  234.5 4.6 %copy-start.4 = (bf16[512,128]{1,0:T(8,128)(2,1)S(1)}, bf16[512,128]{1,0:T(8,128)(2,1)}, u32[]{:S(2)}) copy-start(bf16[512,128]{1,0:T(8,128)(2,1)} %get-tuple-element.329) | copy-start | bytes 393220 | tf_op jit(solution)/shard_map/while
  250.5 4.5 %copy-start.1 = (bf16[128,1,32,192]{0,3,2,1:T(8,128)(2,1)S(1)}, bf16[128,1,32,192]{0,3,2,1:T(8,128)(2,1)}, u32[]{:S(2)}) copy-start(bf16[128,1,32,192]{0,3,2,1:T(8,128)(2,1)} %get-tuple-element.323) | copy-start | bytes 4718596 | tf_op jit(solution)/shard_map/while
  262.8 4.6 %copy-start.3 = (bf16[128,512]{1,0:T(8,128)(2,1)S(1)}, bf16[128,512]{1,0:T(8,128)(2,1)}, u32[]{:S(2)}) copy-start(bf16[128,512]{1,0:T(8,128)(2,1)} %get-tuple-element.327) | copy-start | bytes 393220 | tf_op jit(solution)/shard_map/while
  262.8 4.6 %copy-start.4 = (bf16[512,128]{1,0:T(8,128)(2,1)S(1)}, bf16[512,128]{1,0:T(8,128)(2,1)}, u32[]{:S(2)}) copy-start(bf16[512,128]{1,0:T(8,128)(2,1)} %get-tuple-element.329) | copy-start | bytes 393220 | tf_op jit(solution)/shard_map/while
  278.8 4.5 %copy-start.1 = (bf16[128,1,32,192]{0,3,2,1:T(8,128)(2,1)S(1)}, bf16[128,1,32,192]{0,3,2,1:T(8,128)(2,1)}, u32[]{:S(2)}) copy-start(bf16[128,1,32,192]{0,3,2,1:T(8,128)(2,1)} %get-tuple-element.323) | copy-start | bytes 4718596 | tf_op jit(solution)/shard_map/while
  291.1 4.6 %copy-start.3 = (bf16[128,512]{1,0:T(8,128)(2,1)S(1)}, bf16[128,512]{1,0:T(8,128)(2,1)}, u32[]{:S(2)}) copy-start(bf16[128,512]{1,0:T(8,128)(2,1)} %get-tuple-element.327) | copy-start | bytes 393220 | tf_op jit(solution)/shard_map/while
  291.1 4.6 %copy-start.4 = (bf16[512,128]{1,0:T(8,128)(2,1)S(1)}, bf16[512,128]{1,0:T(8,128)(2,1)}, u32[]{:S(2)}) copy-start(bf16[512,128]{1,0:T(8,128)(2,1)} %get-tuple-element.329) | copy-start | bytes 393220 | tf_op jit(solution)/shard_map/while
Sparse Core Ops, SparseCore 0:
  12.5 94.8 all-gather.1
where the time goes:
time: 305 us; the launch traced here: 304 us
  local copies, waits for them, and re-layouts  109 us (36%)
  matrix products  88.3 us (29%)
  blocking collectives  40.8 us (13%)
  waiting for transfers between devices  27.1 us (9%)
  starting transfers between devices  14.1 us (5%)
  between operations  13.5 us (4%)
  other arithmetic  7.55 us (2%)
  loops' own time  4.31 us (1%)
    reshape x12, local copies, waits for them, and re-layouts, outer_channels(): product.astype(jnp.bfloat16)  70.8 us
    dot_general x12, matrix products, outer_channels(): lax.dot_general(weight, product, (((0,), (1,)), ((), ())), preferred_elem...  51 us
    all_gather x1, blocking collectives, shards(): col_wide = lax.all_gather(local_projected, 'col', axis=3, tiled=True)  40.8 us
    all_to_all x1, waiting for transfers between devices, shards(): lax.all_to_all(col_wide, 'row', split_axis=3, concat_axis=0, tiled=True)  27.1 us
    dot_general x12, matrix products, outer_channels(): lax.dot_general(rows_side, flat_cols, (((0,), (0,)), ((), ())), preferred...  25.5 us
    all_to_all x1, starting transfers between devices, shards(): lax.all_to_all(col_wide, 'row', split_axis=3, concat_axis=0, tiled=True)  14.1 us
    while x4, local copies, waits for them, and re-layouts, shards(): lax.map(pair_block, jnp.arange(row_length // block_size, dtype=jnp.int32))  11.7 us
    dot_general x6, matrix products, finish(): lax.dot_general(w_down, hidden, (((0,), (0,)), ((), ())), preferred_eleme...  10.8 us
  transfers between devices with their start and end apart: 2, of which 1 were waited for; matrix products, arithmetic and copies ran while one was open for 7% of the time, Pallas kernels for 0%

commit v1 on v0

v1 whole, which is shorter than its diff:
```python
import functools

import jax
import jax.numpy as jnp
from jax import lax
from jax.experimental import pallas as pl
from jax.experimental.pallas import tpu as pltpu
from jax.sharding import PartitionSpec as P

EPSILON = 1e-05
VMEM_LIMIT = 60 * 1024 * 1024


def project_kernel(x_ref, gain_ref, bias_ref, w_ref, pbias_ref, x0_ref, x1_ref, y_ref, s0, s1, sy):
    rows = x_ref.shape[0]
    low = lax.broadcasted_iota(jnp.int32, (1, 128), 1) < 64
    w2 = jnp.concatenate([w_ref[...], w_ref[...]], axis=1)
    for s in range(rows):
        x = x_ref[s].astype(jnp.float32)
        mean = jnp.mean(x, axis=-1, keepdims=True)
        cen = x - mean
        var = jnp.mean(cen * cen, axis=-1, keepdims=True)
        normed = (cen * lax.rsqrt(var + EPSILON) * gain_ref[...] + bias_ref[...]).astype(jnp.bfloat16)
        d = jnp.dot(normed, w2, preferred_element_type=jnp.float32) + pbias_ref[...]
        for q in range(4):
            sy[q, :, s, :] = jnp.where(low, d[48 * q : 48 * q + 24], d[48 * q + 24 : 48 * q + 48])
        t0 = d[0:128].T
        s0[:, s, :] = t0[0:64]
        t1 = jnp.concatenate([d[128:192], d[128:192]], axis=0).T
        s1[0:16, s, :] = jnp.where(low, t1[0:16], t1[16:32])
        s1[16:32, s, :] = jnp.where(low, t1[32:48], t1[48:64])
    x0_ref[...] = s0[...].astype(jnp.bfloat16)
    x1_ref[...] = s1[...].astype(jnp.bfloat16)
    y_ref[...] = sy[...].astype(jnp.bfloat16)


def project(x, gain, bias, w, pbias):
    rows = x.shape[0]
    return pl.pallas_call(
        project_kernel,
        out_shape=(
            jax.ShapeDtypeStruct((64, rows, 128), jnp.bfloat16),
            jax.ShapeDtypeStruct((32, rows, 128), jnp.bfloat16),
            jax.ShapeDtypeStruct((4, 24, rows, 128), jnp.bfloat16),
        ),
        scratch_shapes=[
            pltpu.VMEM((64, rows, 128), jnp.float32),
            pltpu.VMEM((32, rows, 128), jnp.float32),
            pltpu.VMEM((4, 24, rows, 128), jnp.float32),
        ],
        name="project",
    )(x, gain[None, :], bias[None, :], w, jnp.concatenate([pbias, pbias])[None, :])


def pair_kernel(
    g0, g1, h, wf, wm, wup, wdn, bout, pg, pb, bup, bdn, out, lf, lm, r1f, r1m, pbuf
):
    step = pl.program_id(0)
    f32, bf16 = jnp.float32, jnp.bfloat16

    @pl.when(step == 0)
    def _():
        low = lax.broadcasted_iota(jnp.int32, (1, 128), 1) < 64
        for p in range(24):
            t = h[p].astype(f32).T.astype(bf16)
            rows = slice(p * 32, p * 32 + 32)
            lf[rows, 0:128] = t[0:32]
            lm[rows, 0:128] = t[32:64]
            lf[rows, 128:256] = t[64:96]
            lm[rows, 128:256] = t[96:128]
        zero = jnp.zeros((128, 128), f32)
        for dst, base in ((r1f, 16), (r1m, 0)):
            for b in range(16):
                q = g1[base + b].astype(f32)
                r = pltpu.roll(q, 64, axis=1)
                dst[b, 0:128] = jnp.where(low, q, zero).astype(bf16)
                dst[b, 128:256] = jnp.where(low, zero, r).astype(bf16)
                dst[b + 16, 0:128] = jnp.where(low, r, zero).astype(bf16)
                dst[b + 16, 128:256] = jnp.where(low, zero, q).astype(bf16)

    base = pl.multiple_of(step * 128, 128)
    for d, (lref, rref, off) in enumerate(((lf, r1f, 32), (lm, r1m, 0))):
        both = lref[pl.ds(base, 128), :]
        lhs0 = jnp.concatenate([both[:, 0:128], both[:, 128:256]], axis=0)
        for bp in range(16):
            b0, b1 = 2 * bp, 2 * bp + 1
            rhs0 = jnp.concatenate([g0[off + b0], g0[off + b1]], axis=1)
            o0 = jnp.dot(lhs0, rhs0, preferred_element_type=f32).astype(bf16)
            rhs1 = jnp.concatenate([rref[b0], rref[b1]], axis=1)
            o1 = jnp.dot(both, rhs1, preferred_element_type=f32).astype(bf16)
            for e, b in enumerate((b0, b1)):
                rows = slice(b * 32, b * 32 + 32)
                lanes = slice(e * 128, e * 128 + 128)
                for i in range(8):
                    pbuf[d, rows, i * 128 : i * 128 + 128] = o0[i * 32 : i * 32 + 32, lanes]
                for i in range(4):
                    pbuf[d, rows, (8 + i) * 128 : (9 + i) * 128] = o1[i * 32 : i * 32 + 32, lanes]

    for n in range(6):
        cols = slice(n * 256, n * 256 + 256)
        zf = jnp.dot(wf[...], pbuf[0, :, cols], preferred_element_type=f32)
        zm = jnp.dot(wm[...], pbuf[1, :, cols], preferred_element_type=f32)
        pair = jnp.maximum(zf + bout[...], 0.0) + jnp.maximum(zm + bout[...], 0.0)
        mean = jnp.mean(pair, axis=0, keepdims=True)
        cen = pair - mean
        var = jnp.mean(cen * cen, axis=0, keepdims=True)
        normed = (cen * lax.rsqrt(var + EPSILON) * pg[...] + pb[...]).astype(bf16)
        hid = jnp.dot(wup[...], normed, preferred_element_type=f32)
        hid = jnp.maximum(hid + bup[...], 0.0).astype(bf16)
        upd = jnp.dot(wdn[...], hid, preferred_element_type=f32)
        res = pair + upd + bdn[...]
        for e in range(2):
            g = 2 * n + e
            t = res[:, e * 128 : e * 128 + 128].T.astype(bf16)
            if g < 8:
                out[g // 4, g % 4, 0:128, :] = t
            else:
                out[0, g - 8, 128:192, :] = t[0:64]
                out[1, g - 8, 128:192, :] = t[64:128]


def pair_block(g0, g1, h, w_out, b_out, pair_gain, pair_bias, w_up, b_up, w_down, b_down):
    scaled = (w_out.astype(jnp.float32) / g0.shape[1]).astype(jnp.bfloat16)
    wf = scaled.reshape(32, 32, 128).transpose(2, 1, 0).reshape(128, 1024)
    wm = scaled.T
    whole = lambda shape: pl.BlockSpec(shape, lambda k: (0,) * len(shape), pipeline_mode=pl.Buffered(1))
    col = lambda v: v[:, None]
    args = (g0, g1, h, wf, wm, w_up.T, w_down.T, col(b_out), col(pair_gain), col(pair_bias), col(b_up), col(b_down))
    out = pl.pallas_call(
        pair_kernel,
        grid=(6,),
        in_specs=[whole(a.shape) for a in args],
        out_specs=pl.BlockSpec((2, 4, 192, 128), lambda k: (0, k, 0, 0)),
        out_shape=jax.ShapeDtypeStruct((2, 24, 192, 128), jnp.bfloat16),
        scratch_shapes=[
            pltpu.VMEM((768, 256), jnp.bfloat16),
            pltpu.VMEM((768, 256), jnp.bfloat16),
            pltpu.VMEM((32, 256, 128), jnp.bfloat16),
            pltpu.VMEM((32, 256, 128), jnp.bfloat16),
            pltpu.VMEM((2, 1024, 1536), jnp.bfloat16),
        ],
        compiler_params=pltpu.CompilerParams(vmem_limit_bytes=VMEM_LIMIT),
        name="pair",
    )(*args)
    return out.reshape(48, 192, 128)


def shards(
    alignment,
    alignment_norm_gain,
    alignment_norm_bias,
    projection_weight,
    projection_bias_pair,
    w_out,
    b_out,
    pair_gain,
    pair_bias,
    w_up,
    b_up,
    w_down,
    b_down,
):
    x0, x1, y = project(
        alignment, alignment_norm_gain, alignment_norm_bias, projection_weight, projection_bias_pair
    )
    g0 = lax.all_gather(x0, "row", axis=1, tiled=True)
    g1 = lax.all_gather(x1, "row", axis=1, tiled=True)
    wide = lax.all_gather(y, "col", axis=0, tiled=True)
    h = lax.all_to_all(wide, "row", split_axis=0, concat_axis=2, tiled=True)[0]
    return pair_block(
        g0, g1, h, w_out, b_out, pair_gain, pair_bias, w_up, b_up, w_down, b_down
    )


def solution(mesh):
    return jax.shard_map(
        shards,
        mesh=mesh,
        in_specs=(P("row", "col", None),) + (P(),) * 12,
        out_specs=P("row", "col", None),
        check_vma=False,
    )
```

time: 305 us -> 198 us (0.65)
  the two profiles are of different devices: /device:TPU:1 before, /device:TPU:12 now
where the time goes in v1:
time: 198 us; the launch traced here: 196 us
  waiting for transfers between devices  74.7 us (38%)
  Pallas kernels  40 us (20%)
  blocking collectives  35.5 us (18%)
  local copies, waits for them, and re-layouts  20.1 us (10%)
  between operations  13.5 us (7%)
  starting transfers between devices  10.2 us (5%)
  other arithmetic  2.17 us (1%)
    all_gather x1, waiting for transfers between devices, shards(): g0 = lax.all_gather(x0, 'row', axis=1, tiled=True)  58.9 us
    pallas_call x1, Pallas kernels, pair_block(): pl.pallas_call(pair_kernel, grid=(6,), in_specs=[whole(a.shape) for a in...  37.4 us
    all_gather x1, blocking collectives, shards(): wide = lax.all_gather(y, 'col', axis=0, tiled=True)  35.5 us
    all_to_all x1, waiting for transfers between devices, shards(): h = lax.all_to_all(wide, 'row', split_axis=0, concat_axis=2, tiled=True)[0]  15.8 us
    all_to_all x1, starting transfers between devices, shards(): h = lax.all_to_all(wide, 'row', split_axis=0, concat_axis=2, tiled=True)[0]  10.1 us
    all_gather x1, local copies, waits for them, and re-layouts, shards(): g0 = lax.all_gather(x0, 'row', axis=1, tiled=True)  4.27 us
  transfers between devices with their start and end apart: 3, of which 2 were waited for; matrix products, arithmetic and copies ran while one was open for 7% of the time, Pallas kernels for 0%

profile of v1, /device:TPU:12, one launch (start us, length us, event | category | flops | bytes accessed | tf_op | source)
XLA Modules:
  0.0 196.0 jit_solution(7343700807582154351)
XLA Ops:
  6.5 0.0 copy-start.4
  6.5 0.0 copy-start.5
  6.5 0.0 copy-start.6
  6.5 0.0 copy-start.7
  6.5 0.0 copy-start.1
  6.5 0.0 copy-start.2
  6.6 0.0 all-gather.5.cloned.1.call-start
  6.6 1.4 maximum_bitcast_fusion.pbias_ref
  8.0 1.5 copy.37.w_ref
  9.5 0.0 copy-start
  9.5 2.6 %project.1 = (bf16[64,4,128]{2,1,0:T(4,128)(2,1)}, bf16[32,4,128]{2,1,0:T(4,128)(2,1)}, bf16[4,24,4,128]{3,2,1,0:T(4,128)(2,1)}) custom-call(bf16[4,192,256]{2,1,0:T(8,128)(2,1)} %x_ref.1, f32[1,256]{1,0:T(1,128)} %bitcast.29, f32[1,256]{1,0:T(1,128)} %bitcast.30, bf16[256,64]{1,0:T(8,128)(2,1)} %copy.37.w_ref, f32[1,128]{1,0:T(1,128)} %maximum_bitcast_fusion.pbias_ref), custom_call_target="tpu_custom_call" | custom-call | tf_op jit(solution)/shard_map/project/pallas_call | solution.py:39
  12.1 1.4 copy.39
  13.4 0.0 all-gather.5.cloned.1.call-update
  13.4 0.0 copy-start.3
  13.5 0.0 all-gather.3.cloned.1.call-start
  13.5 1.5 copy.38
  15.0 0.0 all-gather.3.cloned.1.call-update
  15.0 0.9 copy.40
  15.9 35.5 %all_gather.11 = bf16[32,24,4,128]{3,1,2,0:T(8,128)(2,1)} all-gather(bf16[4,24,4,128]{3,1,2,0:T(8,128)(2,1)S(1)} %copy.40), channel_id=1, replica_groups=mesh['row'=32,'col'=8] {'col'}, dimensions={0}, use_global_device_ids=true | all-gather | bytes 884736 | tf_op jit(solution)/shard_map/all_gather | solution.py:168
  51.4 10.1 %all-to-all-start = ((bf16[32,24,4,128]{3,1,2,0:T(8,128)(2,1)}), bf16[32,24,4,128]{3,1,2,0:T(8,128)(2,1)S(1)}, u32[]{:S(2)}, u32[]{:S(2)}) async-start(bf16[32,24,4,128]{3,1,2,0:T(8,128)(2,1)} %all_gather.11), calls=%async_computation | async-start | bytes 1572864 | tf_op jit(solution)/shard_map/all_to_all | solution.py:169
  61.5 0.0 copy-done.4
  61.5 0.7 copy.50.bout
  62.3 0.0 copy-done.5
  62.3 0.7 copy.51.pg
  63.0 0.0 copy-done.6
  63.0 0.7 copy.52.pb
  63.7 0.0 copy-done.7
  63.7 0.7 copy.54.bdn
  64.5 0.0 copy-done.1
  64.5 0.8 copy.45
  65.2 0.0 copy-done.2
  65.2 0.8 copy.46
  66.0 0.0 copy-done
  66.0 0.1 copy.42
  66.2 0.0 copy-done.3
  66.2 0.9 copy.53.bup
  67.0 0.8 fusion
  67.8 0.2 copy.43
  68.0 0.1 copy.44
  68.1 0.9 copy.49.wf
  69.0 15.8 %all-to-all-done = bf16[32,24,4,128]{3,1,2,0:T(8,128)(2,1)S(1)} async-done(((bf16[32,24,4,128]{3,1,2,0:T(8,128)(2,1)}), bf16[32,24,4,128]{3,1,2,0:T(8,128)(2,1)S(1)}, u32[]{:S(2)}, u32[]{:S(2)}) %all-to-all-start) | async-done | bytes 786464 | tf_op jit(solution)/shard_map/all_to_all | solution.py:169
  84.7 1.3 copy.41
  86.0 0.0 all-gather.5.cloned.1.call-done
  86.0 2.6 %copy.48.g1 = bf16[32,128,128]{2,1,0:T(8,128)(2,1)} copy(bf16[32,128,128]{2,0,1:T(8,128)(2,1)} %all-gather.5.cloned.1.call-done) | data formatting | bytes 2097152 | tf_op jit(solution)/shard_map/all_gather | solution.py:167
  88.7 58.9 %all-gather.3.cloned.1.call-done = bf16[64,128,128]{2,0,1:T(8,128)(2,1)} async-done(((bf16[64,4,128]{2,0,1:T(8,128)(2,1)}), bf16[64,128,128]{2,0,1:T(8,128)(2,1)}) %all-gather.3.cloned.1.call-update) | async-done | bytes 2097168 | tf_op jit(solution)/shard_map/all_gather | solution.py:166
  147.5 4.3 %copy.47.g0 = bf16[64,128,128]{2,1,0:T(8,128)(2,1)} copy(bf16[64,128,128]{2,0,1:T(8,128)(2,1)} %all-gather.3.cloned.1.call-done) | data formatting | bytes 4194304 | tf_op jit(solution)/shard_map/all_gather | solution.py:166
  151.8 37.4 %pair.1 = bf16[2,24,192,128]{3,2,1,0:T(8,128)(2,1)} custom-call(bf16[64,128,128]{2,1,0:T(8,128)(2,1)} %copy.47.g0, bf16[32,128,128]{2,1,0:T(8,128)(2,1)} %copy.48.g1, bf16[24,128,128]{2,1,0:T(8,128)(2,1)} %bitcast.22, bf16[128,1024]{1,0:T(8,128)(2,1)} %copy.49.wf, bf16[128,1024]{1,0:T(8,128)(2,1)} %get-tuple-element.11.wm, bf16[512,128]{1,0:T(8,128)(2,1)} %bitcast.26, ...), custom_call_target="tpu_custom_call" | custom-call | tf_op jit(solution)/shard_map/pair/pallas_call | solution.py:129
Async XLA Ops:
  6.5 55.0 %copy-start.4 = (f32[128]{0:T(128)S(1)}, f32[128]{0:T(128)}, u32[]{:S(2)}) copy-start(f32[128]{0:T(128)} %param.19) | copy-start | bytes 1540
  6.5 55.7 %copy-start.5 = (f32[128]{0:T(128)S(1)}, f32[128]{0:T(128)}, u32[]{:S(2)}) copy-start(f32[128]{0:T(128)} %param.20) | copy-start | bytes 1540
  6.5 56.5 %copy-start.6 = (f32[128]{0:T(128)S(1)}, f32[128]{0:T(128)}, u32[]{:S(2)}) copy-start(f32[128]{0:T(128)} %param.21) | copy-start | bytes 1540
  6.5 57.2 %copy-start.7 = (f32[128]{0:T(128)S(1)}, f32[128]{0:T(128)}, u32[]{:S(2)}) copy-start(f32[128]{0:T(128)} %param.25) | copy-start | bytes 1540
  6.5 57.9 %copy-start.1 = (bf16[128,512]{1,0:T(8,128)(2,1)S(1)}, bf16[128,512]{1,0:T(8,128)(2,1)}, u32[]{:S(2)}) copy-start(bf16[128,512]{1,0:T(8,128)(2,1)} %param.22) | copy-start | bytes 393220
  6.5 58.7 %copy-start.2 = (bf16[512,128]{1,0:T(8,128)(2,1)S(1)}, bf16[512,128]{1,0:T(8,128)(2,1)}, u32[]{:S(2)}) copy-start(bf16[512,128]{1,0:T(8,128)(2,1)} %param.24) | copy-start | bytes 393220
  6.6 79.5 %all-gather.5.cloned.1.call-start = ((), (), s32[]{:S(2)}) async-start(), calls=%async_computation.2 | async-start | bytes 1081344 | tf_op jit(solution)/shard_map/all_gather | solution.py:167
  9.5 56.5 %copy-start = (bf16[1024,128]{1,0:T(8,128)(2,1)S(1)}, bf16[1024,128]{1,0:T(8,128)(2,1)}, u32[]{:S(2)}) copy-start(bf16[1024,128]{1,0:T(8,128)(2,1)} %param.18) | copy-start | bytes 786436
  13.4 52.7 %copy-start.3 = (f32[512]{0:T(512)S(1)}, f32[512]{0:T(512)}, u32[]{:S(2)}) copy-start(f32[512]{0:T(512)} %param.23) | copy-start | bytes 6148
  13.5 134.1 %all-gather.3.cloned.1.call-start = ((), (), s32[]{:S(2)}) async-start(), calls=%async_computation.1 | async-start | bytes 2162688 | tf_op jit(solution)/shard_map/all_gather | solution.py:166
  51.4 33.3 %all-to-all-start = ((bf16[32,24,4,128]{3,1,2,0:T(8,128)(2,1)}), bf16[32,24,4,128]{3,1,2,0:T(8,128)(2,1)S(1)}, u32[]{:S(2)}, u32[]{:S(2)}) async-start(bf16[32,24,4,128]{3,1,2,0:T(8,128)(2,1)} %all_gather.11), calls=%async_computation | async-start | bytes 1572864 | tf_op jit(solution)/shard_map/all_to_all | solution.py:169
Sparse Core Ops, SparseCore 0:
  13.6 66.9 all-gather.4
  82.4 65.1 all-gather.2

commit v2 on v1

v2 whole, which is shorter than its diff:
```python
import functools

import jax
import jax.numpy as jnp
from jax import lax
from jax.experimental import pallas as pl
from jax.experimental.pallas import tpu as pltpu
from jax.sharding import PartitionSpec as P

EPSILON = 1e-05
VMEM_LIMIT = 60 * 1024 * 1024


MESH = pl.DeviceIdType.MESH
ZN, XN = 8, 4


def project_block(x_ref, gain_ref, bias_ref, w_ref, pbias_ref, stage):
    rows = x_ref.shape[0]
    low = lax.broadcasted_iota(jnp.int32, (1, 128), 1) < 64
    w2 = jnp.concatenate([w_ref[...], w_ref[...]], axis=1)
    for s in range(rows):
        x = x_ref[s].astype(jnp.float32)
        mean = jnp.mean(x, axis=-1, keepdims=True)
        cen = x - mean
        var = jnp.mean(cen * cen, axis=-1, keepdims=True)
        normed = (cen * lax.rsqrt(var + EPSILON) * gain_ref[...] + bias_ref[...]).astype(jnp.bfloat16)
        d = jnp.dot(normed, w2, preferred_element_type=jnp.float32) + pbias_ref[...]
        t0 = jnp.concatenate([d[48 * q : 48 * q + 32] for q in range(4)], axis=0).T
        t1 = jnp.concatenate([d[48 * q + 32 : 48 * q + 48] for q in range(4)] * 2, axis=0).T
        for h in range(2):
            stage[h, 0:32, s, :] = t0[32 * h : 32 * h + 32]
            stage[h, 32:48, s, :] = jnp.where(low, t1[32 * h : 32 * h + 16], t1[32 * h + 16 : 32 * h + 32])


def exchange_kernel(
    x_ref, gain_ref, bias_ref, w_ref, pbias_ref, g, hl, hr, stage, block, hstage, hsend,
    own_sem, l_send, l_recv, r_send, r_recv, y_send, y_recv, p_send, p_recv, h_send, h_recv,
):
    bf16, f32 = jnp.bfloat16, jnp.float32
    row, col = lax.axis_index("row"), lax.axis_index("col")
    core = lax.rem(row, 2)
    z = lax.rem(row // 2, ZN)
    ylo = row // (2 * ZN)
    x = lax.rem(col, XN)
    yhi = col // XN

    def row_of(ylo_, z_, core_):
        return (ylo_ * ZN + z_) * 2 + core_

    zup, zdn = lax.rem(z + 1, ZN), lax.rem(z + ZN - 1, ZN)
    up = (row_of(ylo, zup, core), col)
    down = (row_of(ylo, zdn, core), col)
    across = (row_of(1 - ylo, z, core), col)
    partner = (row_of(ylo, z, 1 - core), col)
    xup = (row, yhi * XN + lax.rem(x + 1, XN))
    xdn = (row, yhi * XN + lax.rem(x + XN - 1, XN))
    facing = (row_of(1 - ylo, z, core), (1 - yhi) * XN + x)

    barrier = pltpu.get_barrier_semaphore()
    others = (up, down, across, partner, xup, xdn, facing)
    for dev in others:
        pl.semaphore_signal(barrier, inc=1, device_id=dev, device_id_type=MESH)

    project_block(x_ref, gain_ref, bias_ref, w_ref, pbias_ref, stage)
    block[...] = stage[...].astype(bf16)
    own = [pltpu.make_async_copy(block.at[h], g.at[h, :, row], own_sem.at[h]) for h in range(2)]
    for c in own:
        c.start()
    pl.semaphore_wait(barrier, len(others))

    sent = []

    def slot(h, ylo_, dz, core_):
        return g.at[h, :, row_of(ylo_, lax.rem(z + dz + ZN, ZN), core_)]

    def copy(ref, send, recv, dev):
        c = pltpu.make_async_remote_copy(ref, ref, send, recv, device_id=dev, device_id_type=MESH)
        return c

    def send(ref, s, r, dev):
        c = copy(ref, s, r, dev)
        c.start()
        sent.append(c)

    def arrived(ref, r):
        copy(ref, own_sem.at[0], r, partner).wait_recv()

    def to_partner(h, which, dz, ylo_):
        send(slot(h, ylo_, dz, core), p_send.at[h, which, dz + 3], p_recv.at[h, which, dz + 3], partner)

    def ring_l(which, ylo_, dz):
        top, bottom = (4, 3) if which == 0 else (3, 4)
        ref = slot(0, ylo_, dz, core)
        if dz <= 0 and -dz < top:
            t = -dz
            send(ref, l_send.at[which, 0, t], l_recv.at[which, 0, t], up)
        if dz >= 0 and dz < bottom:
            t = dz
            send(ref, l_send.at[which, 1, t], l_recv.at[which, 1, t], down)

    def ring_r(dz):
        ref = slot(1, ylo, dz, core)
        if dz <= 0 and -dz < 4:
            send(ref, r_send.at[0, -dz], r_recv.at[0, -dz], up)
        if dz >= 0 and dz < 3:
            send(ref, r_send.at[1, dz], r_recv.at[1, dz], down)
        send(ref, y_send.at[1, dz + 4], y_recv.at[1, dz + 4], across)

    def pslot(h, which, ylo_, dz):
        i = (dz + 4) % 8
        send(slot(h, ylo_, dz, core), p_send.at[h, which, i], p_recv.at[h, which, i], partner)

    own[0].wait()
    own[1].wait()
    ring_l(0, ylo, 0)
    send(slot(0, ylo, 0, core), y_send.at[0, 0], y_recv.at[0, 0], across)
    ring_r(0)
    pslot(0, 0, ylo, 0)
    pslot(1, 0, ylo, 0)
    arrived(slot(0, 1 - ylo, 0, core), y_recv.at[0, 0])
    ring_l(1, 1 - ylo, 0)
    pslot(0, 1, 1 - ylo, 0)
    prev = [0]
    for t in range(1, 5):
        for which, ylo_ in ((0, ylo), (1, 1 - ylo)):
            top, bottom = (4, 3) if which == 0 else (3, 4)
            if t <= top:
                arrived(slot(0, ylo_, -t, core), l_recv.at[which, 0, t - 1])
                ring_l(which, ylo_, -t)
                pslot(0, which, ylo_, -t)
            if t <= bottom:
                arrived(slot(0, ylo_, t, core), l_recv.at[which, 1, t - 1])
                ring_l(which, ylo_, t)
                pslot(0, which, ylo_, t)
        now = []
        arrived(slot(1, ylo, -t, core), r_recv.at[0, t - 1])
        ring_r(-t)
        pslot(1, 0, ylo, -t)
        now.append(-t)
        if t <= 3:
            arrived(slot(1, ylo, t, core), r_recv.at[1, t - 1])
            ring_r(t)
            pslot(1, 0, ylo, t)
            now.append(t)
        for dz in prev:
            arrived(slot(1, 1 - ylo, dz, core), y_recv.at[1, dz + 4])
            pslot(1, 1, 1 - ylo, dz)
        prev = now
    for dz in prev:
        arrived(slot(1, 1 - ylo, dz, core), y_recv.at[1, dz + 4])
        pslot(1, 1, 1 - ylo, dz)

    offset = lax.rem(x - z // 2 + XN, XN)
    q = lax.rem(row, 4)
    shift0 = lax.rem(128 - 32 * q, 128)
    shift1 = lax.rem(128 - 32 * q + 64, 128)
    shift2 = lax.rem(128 - 16 * q + 32, 128)
    lane = lax.broadcasted_iota(jnp.int32, (1, 128), 1)
    flat = g.reshape(2, 48, 128, 128)
    for h, dst in ((0, hl), (1, hr)):
        for which in range(2):
            for dz in range(-3, 5):
                i = (dz + 4) % 8
                arrived(slot(h, (ylo, 1 - ylo)[which], dz if dz < 4 else -4, 1 - core), p_recv.at[h, which, i])

        @pl.when(offset == 0)
        def _(h=h, dst=dst):
            for p in range(16):
                a0 = pltpu.roll(flat[h, p].astype(f32), shift0, axis=1)
                a1 = pltpu.roll(flat[h, p + 16].astype(f32), shift1, axis=1)
                b = pltpu.roll(flat[h, 32 + p].astype(f32), shift2, axis=1)
                t = jnp.where(lane < 32, a0, jnp.where((lane >= 64) & (lane < 96), a1, b)).T
                for e in range(2):
                    at = pl.ds(p + 16 * e, 24, stride=32)
                    hstage[0, at, :] = t[64 * e : 64 * e + 24]
                    hstage[1, at, :] = t[64 * e + 24 : 64 * e + 48]
            hsend[h, :, 0:128] = hstage[0].astype(bf16)
            hsend[h, :, 128:256] = hstage[1].astype(bf16)

            @pl.when(ylo == yhi)
            def _():
                c = pltpu.make_async_copy(hsend.at[h], dst, h_recv.at[h])
                c.start()
                c.wait()

            @pl.when(ylo != yhi)
            def _():
                c = pltpu.make_async_remote_copy(
                    hsend.at[h], dst, h_send.at[h, 0], h_recv.at[h], device_id=facing, device_id_type=MESH
                )
                c.start()
                c.wait()

            copy(dst, h_send.at[h, 1], h_recv.at[h], xup).start()
            copy(dst, h_send.at[h, 2], h_recv.at[h], xdn).start()

        @pl.when(offset != 0)
        def _(h=h, dst=dst):
            arrived(dst, h_recv.at[h])

        relay, target = ((1, xup), (3, xdn))[h]

        @pl.when(offset == relay)
        def _(h=h, dst=dst, target=target):
            copy(dst, h_send.at[h, 3], h_recv.at[h], target).start()

    for h, dst in ((0, hl), (1, hr)):
        relay, target = ((1, xup), (3, xdn))[h]

        @pl.when(offset == 0)
        def _(h=h, dst=dst):
            copy(dst, h_send.at[h, 1], h_recv.at[h], xup).wait_send()
            copy(dst, h_send.at[h, 2], h_recv.at[h], xdn).wait_send()

        @pl.when(offset == relay)
        def _(h=h, dst=dst, target=target):
            copy(dst, h_send.at[h, 3], h_recv.at[h], target).wait_send()

    for c in sent:
        c.wait_send()


def exchange(x, gain, bias, w, pbias):
    rows = x.shape[0]
    bf16, f32 = jnp.bfloat16, jnp.float32
    vmem = pl.BlockSpec(memory_space=pltpu.VMEM)
    dma = pltpu.SemaphoreType.DMA
    return pl.pallas_call(
        exchange_kernel,
        in_specs=[vmem] * 5,
        out_specs=[vmem] * 3,
        out_shape=(
            jax.ShapeDtypeStruct((2, 48, 32, rows, 128), bf16),
            jax.ShapeDtypeStruct((768, 256), bf16),
            jax.ShapeDtypeStruct((768, 256), bf16),
        ),
        scratch_shapes=[
            pltpu.VMEM((2, 48, rows, 128), f32),
            pltpu.VMEM((2, 48, rows, 128), bf16),
            pltpu.VMEM((2, 768, 128), f32),
            pltpu.VMEM((2, 768, 256), bf16),
            dma((2,)),
            dma((2, 2, 4)),
            dma((2, 2, 4)),
            dma((2, 4)),
            dma((2, 4)),
            dma((2, 8)),
            dma((2, 8)),
            dma((2, 2, 8)),
            dma((2, 2, 8)),
            dma((2, 4)),
            dma((2,)),
        ],
        compiler_params=pltpu.CompilerParams(
            collective_id=0, has_side_effects=True, vmem_limit_bytes=16 * 1024 * 1024
        ),
        name="exchange",
    )(x, gain[None, :], bias[None, :], w, jnp.concatenate([pbias, pbias])[None, :])


def pair_kernel(
    g, lf, lm, wf, wm, wup, wdn, bout, pg, pb, bup, bdn, out, r1f, r1m, pbuf, zbuf, nbuf, hbuf, obuf,
    bout_b, pg_b, pb_b, bdn_b, bup_b, sem,
):
    f32, bf16 = jnp.float32, jnp.bfloat16
    low = lax.broadcasted_iota(jnp.int32, (1, 128), 1) < 64
    zero = jnp.zeros((128, 128), f32)
    for dst, base in ((r1f, 1), (r1m, 0)):
        for b in range(16):
            q = g[base, 32 + b].astype(f32)
            r = pltpu.roll(q, 64, axis=1)
            dst[b, 0:128] = jnp.where(low, q, zero).astype(bf16)
            dst[b, 128:256] = jnp.where(low, zero, r).astype(bf16)
            dst[b + 16, 0:128] = jnp.where(low, r, zero).astype(bf16)
            dst[b + 16, 128:256] = jnp.where(low, zero, q).astype(bf16)
    for wide, narrow in ((bout_b, bout), (pg_b, pg), (pb_b, pb), (bdn_b, bdn), (bup_b, bup)):
        wide[...] = jnp.broadcast_to(narrow[...], wide.shape)

    def twice(ref, rows=slice(None)):
        v = ref[rows, :]
        return jnp.concatenate([v, v], axis=1)

    def outer_unit(k, d, bp):
        lref, rref, half = ((lf, r1f, 1), (lm, r1m, 0))[d]
        both = lref[pl.ds(pl.multiple_of(k * 128, 128), 128), :]
        lhs0 = jnp.concatenate([both[:, 0:128], both[:, 128:256]], axis=0)
        b0, b1 = 2 * bp, 2 * bp + 1
        rhs0 = jnp.concatenate([g[half, b0], g[half, b1]], axis=1)
        o0 = jnp.dot(lhs0, rhs0, preferred_element_type=f32).astype(bf16)
        rhs1 = jnp.concatenate([rref[b0], rref[b1]], axis=1)
        o1 = jnp.dot(both, rhs1, preferred_element_type=f32).astype(bf16)
        for e, b in enumerate((b0, b1)):
            rows = slice(b * 32, b * 32 + 32)
            lanes = slice(e * 128, e * 128 + 128)
            for i in range(8):
                pbuf[d, rows, i * 128 : i * 128 + 128] = o0[i * 32 : i * 32 + 32, lanes]
            for i in range(4):
                pbuf[d, rows, (8 + i) * 128 : (9 + i) * 128] = o1[i * 32 : i * 32 + 32, lanes]

    def project_chunk(n):
        cols = slice(n * 256, n * 256 + 256)
        b = twice(bout_b)
        zf = jnp.dot(wf[...], pbuf[0, :, cols], preferred_element_type=f32)
        zm = jnp.dot(wm[...], pbuf[1, :, cols], preferred_element_type=f32)
        zbuf[:, cols] = jnp.maximum(zf + b, 0.0) + jnp.maximum(zm + b, 0.0)

    def norm_chunk(n):
        pair = zbuf[:, n * 256 : n * 256 + 256]
        mean = jnp.mean(pair, axis=0, keepdims=True)
        cen = pair - mean
        var = jnp.mean(cen * cen, axis=0, keepdims=True)
        nbuf[n % 2] = (cen * lax.rsqrt(var + EPSILON) * twice(pg_b) + twice(pb_b)).astype(bf16)

    def up_chunk(n, part):
        rows = slice(part * 128, part * 128 + 128)
        hid = jnp.dot(wup[rows, :], nbuf[n % 2], preferred_element_type=f32)
        hbuf[n % 2, rows, :] = jnp.maximum(hid + twice(bup_b, rows), 0.0).astype(bf16)

    def down_chunk(n, slot):
        upd = jnp.dot(wdn[...], hbuf[n % 2], preferred_element_type=f32)
        res = zbuf[:, n * 256 : n * 256 + 256] + upd + twice(bdn_b)
        for e in range(2):
            c = 2 * n + e
            t = res[:, e * 128 : e * 128 + 128].T.astype(bf16)
            for q in range(4):
                if c < 8:
                    obuf[slot, c // 4, c % 4, 48 * q : 48 * q + 32, :] = t[32 * q : 32 * q + 32]
                else:
                    obuf[slot, 0, c - 8, 48 * q + 32 : 48 * q + 48, :] = t[16 * q : 16 * q + 16]
                    obuf[slot, 1, c - 8, 48 * q + 32 : 48 * q + 48, :] = t[64 + 16 * q : 80 + 16 * q]

    def transition(slot):
        stages = []
        for n in range(6):
            stages.append(functools.partial(norm_chunk, n))
            for part in range(4):
                stages.append(functools.partial(up_chunk, n, part))
            stages.append(functools.partial(down_chunk, n, slot))
        return stages

    def outer(k):
        return [functools.partial(outer_unit, k, d, bp) for d in range(2) for bp in range(16)]

    def store(k, slot):
        return [
            pltpu.make_async_copy(obuf.at[slot, w], out.at[w, pl.ds(4 * k, 4)], sem.at[slot, w])
            for w in range(2)
        ]

    for unit in outer(0):
        unit()
    for n in range(6):
        project_chunk(n)

    def body(k, carry):
        slot = lax.rem(k + 1, 2)

        @pl.when(k >= 3)
        def _():
            for c in store(k - 3, slot):
                c.wait()

        units, stages = outer(k), transition(slot)
        done = 0
        for i, unit in enumerate(units):
            unit()
            while done < (i + 1) * len(stages) // len(units):
                stages[done]()
                done += 1
        for c in store(k - 1, slot):
            c.start()
        for n in range(6):
            project_chunk(n)
        return carry

    lax.fori_loop(1, 6, body, 0)
    for c in store(3, 1):
        c.wait()
    for stage in transition(1):
        stage()
    for c in store(5, 1):
        c.start()
    for k, slot in ((4, 0), (5, 1)):
        for c in store(k, slot):
            c.wait()


def pair_block(g, hl, hr, w_out, b_out, pair_gain, pair_bias, w_up, b_up, w_down, b_down):
    bf16, f32 = jnp.bfloat16, jnp.float32
    scaled = (w_out.astype(jnp.float32) / g.shape[2]).astype(jnp.bfloat16)
    wf = scaled.reshape(32, 32, 128).transpose(2, 1, 0).reshape(128, 1024)
    wm = scaled.T
    col = lambda v: v[:, None]
    args = (g, hl, hr, wf, wm, w_up.T, w_down.T, col(b_out), col(pair_gain), col(pair_bias), col(b_up), col(b_down))
    out = pl.pallas_call(
        pair_kernel,
        in_specs=[pl.BlockSpec(memory_space=pltpu.VMEM) for a in args],
        out_specs=pl.BlockSpec(memory_space=pl.ANY),
        out_shape=jax.ShapeDtypeStruct((2, 24, 192, 128), jnp.bfloat16),
        scratch_shapes=[
            pltpu.VMEM((32, 256, 128), bf16),
            pltpu.VMEM((32, 256, 128), bf16),
            pltpu.VMEM((2, 1024, 1536), bf16),
            pltpu.VMEM((128, 1536), f32),
            pltpu.VMEM((2, 128, 256), bf16),
            pltpu.VMEM((2, 512, 256), bf16),
            pltpu.VMEM((2, 2, 4, 192, 128), bf16),
            pltpu.VMEM((128, 128), f32),
            pltpu.VMEM((128, 128), f32),
            pltpu.VMEM((128, 128), f32),
            pltpu.VMEM((128, 128), f32),
            pltpu.VMEM((512, 128), f32),
            pltpu.SemaphoreType.DMA((2, 2)),
        ],
        compiler_params=pltpu.CompilerParams(vmem_limit_bytes=VMEM_LIMIT),
        name="pair",
    )(*args)
    return out.reshape(48, 192, 128)


def shards(
    alignment,
    alignment_norm_gain,
    alignment_norm_bias,
    projection_weight,
    projection_bias_pair,
    w_out,
    b_out,
    pair_gain,
    pair_bias,
    w_up,
    b_up,
    w_down,
    b_down,
):
    g, hl, hr = exchange(
        alignment, alignment_norm_gain, alignment_norm_bias, projection_weight, projection_bias_pair
    )
    g = g.reshape(2, 48, 128, 128)
    return pair_block(
        g, hl, hr, w_out, b_out, pair_gain, pair_bias, w_up, b_up, w_down, b_down
    )


def solution(mesh):
    return jax.shard_map(
        shards,
        mesh=mesh,
        in_specs=(P("row", "col", None),) + (P(),) * 12,
        out_specs=P("row", "col", None),
        check_vma=False,
    )
```

time: 198 us -> 107 us (0.54)
  waiting for transfers between devices: 74.7 us -> 0 us
  Pallas kernels: 40 us -> 88 us
  blocking collectives: 35.5 us -> 0 us
  between operations: 13.5 us -> 0.21 us
  starting transfers between devices: 10.2 us -> 0 us
  local copies, waits for them, and re-layouts: 20.1 us -> 16.6 us
    all_gather x2 -> x0, waiting for transfers between devices: 58.9 us -> none  [the longest x1 58.9 us: shards(): g0 = lax.all_gather(x0, 'row', axis=1, tiled=True)]
    pallas_call x2, Pallas kernels: 40 us -> 88 us  [the longest x1 62.5 us: exchange(): pl.pallas_call(exchange_kernel, in_specs=[vmem] * 5, out_specs=[vmem] * 3...]
    all_gather x1 -> x0, blocking collectives: 35.5 us -> none  [shards(): wide = lax.all_gather(y, 'col', axis=0, tiled=True)]
    all_to_all x1 -> x0, waiting for transfers between devices: 15.8 us -> none  [shards(): h = lax.all_to_all(wide, 'row', split_axis=0, concat_axis=2, tiled=True)[0]]
    all_to_all x1 -> x0, starting transfers between devices: 10.1 us -> none  [shards(): h = lax.all_to_all(wide, 'row', split_axis=0, concat_axis=2, tiled=True)[0]]
    all_gather x2 -> x0, local copies, waits for them, and re-layouts: 6.88 us -> none  [the longest x1 4.27 us: shards(): g0 = lax.all_gather(x0, 'row', axis=1, tiled=True)]
    unnamed x20 -> x16, local copies, waits for them, and re-layouts: 3.19 us -> 8.41 us
    pallas_call x3 -> x0, local copies, waits for them, and re-layouts: 3.75 us -> none  [project(): pl.pallas_call(project_kernel, out_shape=(jax.ShapeDtypeStruct((64, rows,...]
  transfers between devices with their start and end apart: 3 -> 0, of which waited for: 2 -> 0; matrix products, arithmetic and copies ran while one was open for 7% -> 0% of each run, Pallas kernels for 0% -> 0%
where the time goes in v2:
time: 107 us; the launch traced here: 106 us
  Pallas kernels  88 us (82%)
  local copies, waits for them, and re-layouts  16.6 us (16%)
  other arithmetic  1.54 us (1%)
    pallas_call x1, Pallas kernels, exchange(): pl.pallas_call(exchange_kernel, in_specs=[vmem] * 5, out_specs=[vmem] * 3...  62.5 us
    pallas_call x1, Pallas kernels, pair_block(): pl.pallas_call(pair_kernel, in_specs=[pl.BlockSpec(memory_space=pltpu.VME...  25.4 us
    unnamed x16, local copies, waits for them, and re-layouts  8.41 us
    broadcast_in_dim x5, local copies, waits for them, and re-layouts, pair_block(): col = lambda v: v[:, None]  7.05 us

profile of v2, /device:TPU:12, one launch (start us, length us, event | category | flops | bytes accessed | tf_op | source)
XLA Modules:
  0.0 106.3 jit_solution(7669836680667761345)
XLA Ops:
  0.0 0.0 copy-start.5
  0.0 0.0 copy-start.4
  0.0 0.0 copy-start.1
  0.0 0.8 maximum_bitcast_fusion.pbias_ref
  0.8 0.9 copy.23.w_ref
  1.7 1.4 %copy.30.bout = f32[128,1]{1,0:T(8,128)} copy(f32[128,1]{0,1:T(1,128)} %bitcast.27) | data formatting | bytes 1024 | tf_op jit(solution)/shard_map/broadcast_in_dim | solution.py:394
  3.1 1.4 %copy.31.pg = f32[128,1]{1,0:T(8,128)} copy(f32[128,1]{0,1:T(1,128)} %bitcast.28) | data formatting | bytes 1024 | tf_op jit(solution)/shard_map/broadcast_in_dim | solution.py:394
  4.4 1.4 %copy.32.pb = f32[128,1]{1,0:T(8,128)} copy(f32[128,1]{0,1:T(1,128)} %bitcast.29) | data formatting | bytes 1024 | tf_op jit(solution)/shard_map/broadcast_in_dim | solution.py:394
  5.8 1.4 %copy.34.bdn = f32[128,1]{1,0:T(8,128)} copy(f32[128,1]{0,1:T(1,128)} %bitcast.30) | data formatting | bytes 1024 | tf_op jit(solution)/shard_map/broadcast_in_dim | solution.py:394
  7.2 1.7 %copy.27 = bf16[128,512]{0,1:T(8,128)(2,1)} copy(bf16[128,512]{1,0:T(8,128)(2,1)} %param.22) | data formatting | bytes 262144 | tf_op args[9]
  8.9 1.7 %copy.28 = bf16[512,128]{0,1:T(8,128)(2,1)} copy(bf16[512,128]{1,0:T(8,128)(2,1)} %param.24) | data formatting | bytes 262144 | tf_op args[11]
  10.5 1.1 %copy.24 = bf16[1024,128]{0,1:T(8,128)(2,1)S(1)} copy(bf16[1024,128]{1,0:T(8,128)(2,1)} %param.18) | data formatting | bytes 524288 | tf_op args[5]
  11.6 1.5 %copy.33.bup = f32[512,1]{1,0:T(8,128)} copy(f32[512,1]{0,1:T(1,128)} %bitcast.26) | data formatting | bytes 4096 | tf_op jit(solution)/shard_map/broadcast_in_dim | solution.py:394
  13.2 0.7 fusion
  13.9 0.2 copy.25
  14.1 0.1 copy.26
  14.2 0.9 copy.29.wf
  15.0 0.0 copy-done.5
  15.0 0.0 copy-done.4
  15.0 0.0 copy-done.1
  15.0 62.5 %exchange.1 = (bf16[2,48,32,4,128]{4,3,2,1,0:T(4,128)(2,1)S(1)}, bf16[768,256]{1,0:T(8,128)(2,1)S(1)}, bf16[768,256]{1,0:T(8,128)(2,1)S(1)}) custom-call(bf16[4,192,256]{2,1,0:T(8,128)(2,1)S(1)} %copy-done.1, f32[1,256]{1,0:T(1,128)S(1)} %bitcast.20, f32[1,256]{1,0:T(1,128)S(1)} %bitcast.21, bf16[256,64]{1,0:T(8,128)(2,1)S(1)} %copy.23.w_ref, ...), custom_call_target="tpu_custom_call" | custom-call | tf_op jit(solution)/shard_map/exchange/pallas_call | solution.py:229
  77.6 0.0 copy-start
  77.6 1.6 %copy-done = bf16[2,48,32,4,128]{4,3,2,1,0:T(4,128)(2,1)} copy-done((bf16[2,48,32,4,128]{4,3,2,1,0:T(4,128)(2,1)}, bf16[2,48,32,4,128]{4,3,2,1,0:T(4,128)(2,1)S(1)}, u32[]{:S(2)}) %copy-start) | copy-done | bytes 3145752
  79.2 0.0 copy-start.2
  79.2 0.7 copy-done.2
  80.0 0.0 copy-start.3
  80.0 0.7 copy-done.3
  80.7 25.4 %pair.1 = bf16[2,24,192,128]{3,2,1,0:T(8,128)(2,1)} custom-call(bf16[2,48,128,128]{3,2,1,0:T(8,128)(2,1)} %bitcast.19, bf16[768,256]{1,0:T(8,128)(2,1)} %copy-done.2, bf16[768,256]{1,0:T(8,128)(2,1)} %copy-done.3, bf16[128,1024]{1,0:T(8,128)(2,1)} %copy.29.wf, bf16[128,1024]{1,0:T(8,128)(2,1)} %get-tuple-element.11.wm, bf16[512,128]{1,0:T(8,128)(2,1)} %bitcast.24, ...), custom_call_target="tpu_custom_call" | custom-call | tf_op jit(solution)/shard_map/pair/pallas_call | solution.py:396
Async XLA Ops:
  0.0 15.0 %copy-start.5 = (f32[256]{0:T(256)S(1)}, f32[256]{0:T(256)}, u32[]{:S(2)}) copy-start(f32[256]{0:T(256)} %param.15) | copy-start | bytes 3076
  0.0 15.0 %copy-start.4 = (f32[256]{0:T(256)S(1)}, f32[256]{0:T(256)}, u32[]{:S(2)}) copy-start(f32[256]{0:T(256)} %param.14) | copy-start | bytes 3076
  0.0 15.0 %copy-start.1 = (bf16[4,192,256]{2,1,0:T(8,128)(2,1)S(1)}, bf16[4,192,256]{2,1,0:T(8,128)(2,1)}, u32[]{:S(2)}) copy-start(bf16[4,192,256]{2,1,0:T(8,128)(2,1)} %x_ref.1) | copy-start | bytes 1179652
  77.6 1.6 %copy-start = (bf16[2,48,32,4,128]{4,3,2,1,0:T(4,128)(2,1)}, bf16[2,48,32,4,128]{4,3,2,1,0:T(4,128)(2,1)S(1)}, u32[]{:S(2)}) copy-start(bf16[2,48,32,4,128]{4,3,2,1,0:T(4,128)(2,1)S(1)} %get-tuple-element.8) | copy-start | bytes 9437188
  79.2 0.7 copy-start.2
  80.0 0.7 copy-start.3

commit v3 on v2

v3 whole, which is shorter than its diff:
```python
import functools

import jax
import jax.numpy as jnp
from jax import lax
from jax.experimental import pallas as pl
from jax.experimental.pallas import tpu as pltpu
from jax.sharding import PartitionSpec as P

EPSILON = 1e-05
VMEM_LIMIT = 60 * 1024 * 1024


MESH = pl.DeviceIdType.MESH
ZN, XN = 8, 4


def project_block(x_ref, gain_ref, bias_ref, w_ref, pbias_ref, stage):
    rows = x_ref.shape[0]
    low = lax.broadcasted_iota(jnp.int32, (1, 128), 1) < 64
    w2 = jnp.concatenate([w_ref[...], w_ref[...]], axis=0)
    pbias = jnp.concatenate([pbias_ref[...], pbias_ref[...]], axis=1)
    for s in range(rows):
        x = x_ref[s].astype(jnp.float32)
        mean = jnp.mean(x, axis=-1, keepdims=True)
        cen = x - mean
        var = jnp.mean(cen * cen, axis=-1, keepdims=True)
        normed = (cen * lax.rsqrt(var + EPSILON) * gain_ref[...] + bias_ref[...]).astype(jnp.bfloat16)
        d = lax.dot_general(normed, w2, (((1,), (1,)), ((), ())), preferred_element_type=jnp.float32)
        d = d + pbias
        t0 = jnp.concatenate([d[48 * q : 48 * q + 32] for q in range(4)], axis=0).T
        t1 = jnp.concatenate([d[48 * q + 32 : 48 * q + 48] for q in range(4)] * 2, axis=0).T
        for h in range(2):
            stage[h, 0:32, s, :] = t0[32 * h : 32 * h + 32]
            stage[h, 32:48, s, :] = jnp.where(low, t1[32 * h : 32 * h + 16], t1[32 * h + 16 : 32 * h + 32])


def fused_kernel(
    x_ref, gain_ref, bias_ref, w_ref, pbias_ref, w_out, bout, pg, pb, w_up, bup, w_down, bdn, out,
    g, hl, hr, stage, block, hstage, hsend, r1f, r1m, pbuf, zbuf, nbuf, hbuf, wtmp,
    wf, wm, wup, wdn, bout_b, pg_b, pb_b, bdn_b, bup_b,
    own_sem, l_send, l_recv, r_send, r_recv, y_send, y_recv, p_send, p_recv, hs_sem, hf_sem, h_recv,
):
    bf16, f32 = jnp.bfloat16, jnp.float32

    def prepare_weights():
        total = 4 * 32
        wtmp[...] = w_out[...].astype(f32) * (1.0 / total)
        for m in range(8):
            rows = slice(m * 128, m * 128 + 128)
            wm[:, rows] = wtmp[rows, :].T.astype(bf16)
            picked = [wtmp[pl.ds(4 * m + e, 32, stride=32), :] for e in range(4)]
            wf[:, rows] = jnp.concatenate(picked, axis=0).T.astype(bf16)
        for m in range(4):
            rows = slice(m * 128, m * 128 + 128)
            wup[rows, :] = w_up[:, rows].astype(f32).T.astype(bf16)
            wdn[:, rows] = w_down[rows, :].astype(f32).T.astype(bf16)
            bup_b[rows, :] = jnp.broadcast_to(bup[:, rows], (128, 128)).T
        for wide, narrow in ((bout_b, bout), (pg_b, pg), (pb_b, pb), (bdn_b, bdn)):
            wide[...] = jnp.broadcast_to(narrow[...], (128, 128)).T

    row, col = lax.axis_index("row"), lax.axis_index("col")
    core = lax.rem(row, 2)
    z = lax.rem(row // 2, ZN)
    ylo = row // (2 * ZN)
    x = lax.rem(col, XN)
    yhi = col // XN

    def row_of(ylo_, z_, core_):
        return (ylo_ * ZN + z_) * 2 + core_

    zup, zdn = lax.rem(z + 1, ZN), lax.rem(z + ZN - 1, ZN)
    up = (row_of(ylo, zup, core), col)
    down = (row_of(ylo, zdn, core), col)
    across = (row_of(1 - ylo, z, core), col)
    partner = (row_of(ylo, z, 1 - core), col)
    xup = (row, yhi * XN + lax.rem(x + 1, XN))
    xdn = (row, yhi * XN + lax.rem(x + XN - 1, XN))
    facing = (row_of(1 - ylo, z, core), (1 - yhi) * XN + x)

    barrier = pltpu.get_barrier_semaphore()
    others = (up, down, across, partner, xup, xdn, facing)
    for dev in others:
        pl.semaphore_signal(barrier, inc=1, device_id=dev, device_id_type=MESH)

    project_block(x_ref, gain_ref, bias_ref, w_ref, pbias_ref, stage)
    block[...] = stage[...].astype(bf16)
    own = [pltpu.make_async_copy(block.at[h], g.at[h, :, row], own_sem.at[h]) for h in range(2)]
    for c in own:
        c.start()
    pl.semaphore_wait(barrier, len(others))

    sent = []

    def slot(h, ylo_, dz, core_):
        return g.at[h, :, row_of(ylo_, lax.rem(z + dz + ZN, ZN), core_)]

    def copy(ref, send, recv, dev):
        c = pltpu.make_async_remote_copy(ref, ref, send, recv, device_id=dev, device_id_type=MESH)
        return c

    def send(ref, s, r, dev):
        c = copy(ref, s, r, dev)
        c.start()
        sent.append(c)

    def arrived(ref, r):
        copy(ref, own_sem.at[0], r, partner).wait_recv()

    def ring_l(which, ylo_, dz):
        top, bottom = (4, 3) if which == 0 else (3, 4)
        ref = slot(0, ylo_, dz, core)
        if dz <= 0 and -dz < top:
            t = -dz
            send(ref, l_send.at[which, 0, t], l_recv.at[which, 0, t], up)
        if dz >= 0 and dz < bottom:
            t = dz
            send(ref, l_send.at[which, 1, t], l_recv.at[which, 1, t], down)

    def ring_r(dz):
        ref = slot(1, ylo, dz, core)
        if dz <= 0 and -dz < 4:
            send(ref, r_send.at[0, -dz], r_recv.at[0, -dz], up)
        if dz >= 0 and dz < 3:
            send(ref, r_send.at[1, dz], r_recv.at[1, dz], down)
        send(ref, y_send.at[1, dz + 4], y_recv.at[1, dz + 4], across)

    def pslot(h, which, ylo_, dz):
        i = (dz + 4) % 8
        send(slot(h, ylo_, dz, core), p_send.at[h, which, i], p_recv.at[h, which, i], partner)

    own[0].wait()
    own[1].wait()
    ring_l(0, ylo, 0)
    send(slot(0, ylo, 0, core), y_send.at[0, 0], y_recv.at[0, 0], across)
    ring_r(0)
    pslot(0, 0, ylo, 0)
    pslot(1, 0, ylo, 0)
    prepare_weights()
    arrived(slot(0, 1 - ylo, 0, core), y_recv.at[0, 0])
    ring_l(1, 1 - ylo, 0)
    pslot(0, 1, 1 - ylo, 0)
    prev = [0]
    for t in range(1, 5):
        for dz in (-t, t):
            if dz == 4:
                continue
            way = 0 if dz < 0 else 1
            arrived(slot(0, ylo, dz, core), l_recv.at[0, way, t - 1])
            ring_l(0, ylo, dz)
            arrived(slot(1, ylo, dz, core), r_recv.at[way, t - 1])
            ring_r(dz)
            pslot(0, 0, ylo, dz)
            pslot(1, 0, ylo, dz)
        for dz in (-t, t):
            if dz == -4:
                continue
            way = 0 if dz < 0 else 1
            arrived(slot(0, 1 - ylo, dz, core), l_recv.at[1, way, t - 1])
            ring_l(1, 1 - ylo, dz)
            pslot(0, 1, 1 - ylo, dz)
        for dz in prev:
            arrived(slot(1, 1 - ylo, dz, core), y_recv.at[1, dz + 4])
            pslot(1, 1, 1 - ylo, dz)
        prev = [dz for dz in (-t, t) if dz != 4]
    for dz in prev:
        arrived(slot(1, 1 - ylo, dz, core), y_recv.at[1, dz + 4])
        pslot(1, 1, 1 - ylo, dz)

    offset = lax.rem(x - z // 2 + XN, XN)
    q = lax.rem(row, 4)
    shift0 = lax.rem(128 - 32 * q, 128)
    shift1 = lax.rem(128 - 32 * q + 64, 128)
    shift2 = lax.rem(128 - 16 * q + 32, 128)
    lane = lax.broadcasted_iota(jnp.int32, (1, 128), 1)
    flat = g.reshape(2, 48, 128, 128)
    self_source = (offset == 0) & (ylo == yhi)
    far_source = (offset == 0) & (ylo != yhi)

    def chunk(ref, k):
        return ref.at[pl.ds(pl.multiple_of(k * 128, 128), 128)]

    def local(h, dst, k):
        return pltpu.make_async_copy(chunk(hsend.at[h], k), chunk(dst, k), h_recv.at[h, k])

    def first(h, dst, k):
        return pltpu.make_async_remote_copy(
            chunk(hsend.at[h], k), chunk(dst, k), hs_sem.at[h, k], h_recv.at[h, k], device_id=facing, device_id_type=MESH
        )

    def onward(h, dst, k, way):
        return copy(chunk(dst, k), hf_sem.at[h, way, k], h_recv.at[h, k], (xup, xdn)[way])

    def make_rows(h, dst):
        for p in range(16):
            a0 = pltpu.roll(flat[h, p].astype(f32), shift0, axis=1)
            a1 = pltpu.roll(flat[h, p + 16].astype(f32), shift1, axis=1)
            b = pltpu.roll(flat[h, 32 + p].astype(f32), shift2, axis=1)
            t = jnp.where(lane < 32, a0, jnp.where((lane >= 64) & (lane < 96), a1, b)).T
            for e in range(2):
                at = pl.ds(p + 16 * e, 24, stride=32)
                hstage[0, at, :] = t[64 * e : 64 * e + 24]
                hstage[1, at, :] = t[64 * e + 24 : 64 * e + 48]
        hsend[h, :, 0:128] = hstage[0].astype(bf16)
        hsend[h, :, 128:256] = hstage[1].astype(bf16)

        @pl.when(ylo == yhi)
        def _():
            for k in range(6):
                local(h, dst, k).start()

        @pl.when(ylo != yhi)
        def _():
            for k in range(6):
                first(h, dst, k).start()

    def onward_root(h, dst, k):
        @pl.when(offset == 0)
        def _():
            local(h, dst, k).wait()
            onward(h, dst, k, 0).start()
            onward(h, dst, k, 1).start()

    def onward_side(h, dst, k):
        @pl.when((offset == 1) | (offset == 3))
        def _():
            local(h, dst, k).wait()

        @pl.when((offset == 1) & (lax.rem(k, 2) == 0))
        def _():
            onward(h, dst, k, 0).start()

        @pl.when((offset == 3) & (lax.rem(k, 2) == 1))
        def _():
            onward(h, dst, k, 1).start()

    def onward_far(h, dst, k):
        @pl.when(offset == 2)
        def _():
            local(h, dst, k).wait()

    def partner_arrived(h):
        for which in range(2):
            for dz in range(-4, 4):
                at = dz if which == 0 or dz > -4 else 4
                arrived(slot(h, (ylo, 1 - ylo)[which], at, 1 - core), p_recv.at[h, which, (at + 4) % 8])

    low = lane < 64
    zero = jnp.zeros((128, 128), f32)

    def spread(h, dst):
        for b in range(16):
            q_ = flat[h, 32 + b].astype(f32)
            r_ = pltpu.roll(q_, 64, axis=1)
            dst[b, 0:128] = jnp.where(low, q_, zero).astype(bf16)
            dst[b, 128:256] = jnp.where(low, zero, r_).astype(bf16)
            dst[b + 16, 0:128] = jnp.where(low, r_, zero).astype(bf16)
            dst[b + 16, 128:256] = jnp.where(low, zero, q_).astype(bf16)

    def twice(ref, rows=slice(None)):
        v = ref[rows, :]
        return jnp.concatenate([v, v], axis=1)

    def outer_unit(k, d, bp):
        lref, rref, half = ((hl, r1f, 1), (hr, r1m, 0))[d]
        both = lref[pl.ds(pl.multiple_of(k * 128, 128), 128), :]
        lhs0 = jnp.concatenate([both[:, 0:128], both[:, 128:256]], axis=0)
        b0, b1 = 2 * bp, 2 * bp + 1
        rhs0 = jnp.concatenate([flat[half, b0], flat[half, b1]], axis=1)
        o0 = jnp.dot(lhs0, rhs0, preferred_element_type=f32).astype(bf16)
        rhs1 = jnp.concatenate([rref[b0], rref[b1]], axis=1)
        o1 = jnp.dot(both, rhs1, preferred_element_type=f32).astype(bf16)
        for e, b in enumerate((b0, b1)):
            rows = slice(b * 32, b * 32 + 32)
            lanes = slice(e * 128, e * 128 + 128)
            for i in range(8):
                pbuf[rows, i * 128 : i * 128 + 128] = o0[i * 32 : i * 32 + 32, lanes]
            for i in range(4):
                pbuf[rows, (8 + i) * 128 : (9 + i) * 128] = o1[i * 32 : i * 32 + 32, lanes]

    def project_chunk(k, d, n):
        cols = slice(n * 256, n * 256 + 256)
        z_ = jnp.dot((wf, wm)[d][...], pbuf[:, cols], preferred_element_type=f32)
        z_ = jnp.maximum(z_ + twice(bout_b), 0.0)
        zbuf[k, :, cols] = z_ if d == 0 else zbuf[k, :, cols] + z_

    def norm_chunk(k, n):
        pair = zbuf[k, :, n * 256 : n * 256 + 256]
        mean = jnp.mean(pair, axis=0, keepdims=True)
        cen = pair - mean
        var = jnp.mean(cen * cen, axis=0, keepdims=True)
        nbuf[n % 2] = (cen * lax.rsqrt(var + EPSILON) * twice(pg_b) + twice(pb_b)).astype(bf16)

    def up_chunk(n, part):
        rows = slice(part * 128, part * 128 + 128)
        hid = jnp.dot(wup[rows, :], nbuf[n % 2], preferred_element_type=f32)
        hbuf[n % 2, rows, :] = jnp.maximum(hid + twice(bup_b, rows), 0.0).astype(bf16)

    def down_chunk(k, n):
        upd = jnp.dot(wdn[...], hbuf[n % 2], preferred_element_type=f32)
        res = zbuf[k, :, n * 256 : n * 256 + 256] + upd + twice(bdn_b)
        for e in range(2):
            c = 2 * n + e
            t = res[:, e * 128 : e * 128 + 128].T.astype(bf16)
            for q_ in range(4):
                if c < 8:
                    out[c // 4, 4 * k + c % 4, 48 * q_ : 48 * q_ + 32, :] = t[32 * q_ : 32 * q_ + 32]
                else:
                    out[0, 4 * k + c - 8, 48 * q_ + 32 : 48 * q_ + 48, :] = t[16 * q_ : 16 * q_ + 16]
                    out[1, 4 * k + c - 8, 48 * q_ + 32 : 48 * q_ + 48, :] = t[64 + 16 * q_ : 80 + 16 * q_]

    def transition(k):
        stages = []
        for n in range(6):
            stages.append(functools.partial(norm_chunk, k, n))
            for part in range(4):
                stages.append(functools.partial(up_chunk, n, part))
            stages.append(functools.partial(down_chunk, k, n))
        return stages

    partner_arrived(0)

    @pl.when(offset == 0)
    def _():
        make_rows(0, hl)

    partner_arrived(1)

    @pl.when(offset == 0)
    def _():
        onward_root(0, hl, 0)
        make_rows(1, hr)

    spread(1, r1f)
    spread(0, r1m)
    onward_side(0, hl, 0)
    onward_far(0, hl, 0)

    def left_pass(k, carry):
        for bp in range(16):
            outer_unit(k, 0, bp)

        @pl.when(k < 5)
        def _():
            onward_root(0, hl, k + 1)
            onward_side(0, hl, k + 1)
            onward_far(0, hl, k + 1)

        @pl.when(k >= 1)
        def _():
            onward_root(1, hr, k - 1)

        @pl.when(k >= 3)
        def _():
            onward_side(1, hr, k - 3)

        for n in range(6):
            project_chunk(k, 0, n)
        return carry

    lax.fori_loop(0, 6, left_pass, 0)

    onward_far(1, hr, 0)
    for bp in range(16):
        outer_unit(0, 1, bp)
    onward_root(1, hr, 5)
    onward_side(1, hr, 3)
    for n in range(6):
        project_chunk(0, 1, n)

    def right_pass(k, carry):
        onward_far(1, hr, k)
        stages = transition(k - 1)
        done = 0
        for bp in range(16):
            outer_unit(k, 1, bp)
            while done < (bp + 1) * len(stages) // 16:
                stages[done]()
                done += 1

        @pl.when(k < 3)
        def _():
            onward_side(1, hr, k + 3)

        for n in range(6):
            project_chunk(k, 1, n)
        return carry

    lax.fori_loop(1, 6, right_pass, 0)
    for stage_ in transition(5):
        stage_()

    for h, dst in ((0, hl), (1, hr)):
        for k in range(6):

            @pl.when(far_source)
            def _(h=h, dst=dst, k=k):
                first(h, dst, k).wait_send()

            @pl.when(offset == 0)
            def _(h=h, dst=dst, k=k):
                onward(h, dst, k, 0).wait_send()
                onward(h, dst, k, 1).wait_send()

            @pl.when(offset == (1, 3)[k % 2])
            def _(h=h, dst=dst, k=k):
                onward(h, dst, k, k % 2).wait_send()

    for c in sent:
        c.wait_send()


def fused(x, *params):
    rows = x.shape[0]
    bf16, f32 = jnp.bfloat16, jnp.float32
    vmem = pl.BlockSpec(memory_space=pltpu.VMEM)
    dma = pltpu.SemaphoreType.DMA
    args = (x,) + tuple(p[None, :] if p.ndim == 1 else p for p in params)
    out = pl.pallas_call(
        fused_kernel,
        in_specs=[vmem] * len(args),
        out_specs=vmem,
        out_shape=jax.ShapeDtypeStruct((2, 24, 192, 128), bf16),
        scratch_shapes=[
            pltpu.VMEM((2, 48, 32, rows, 128), bf16),
            pltpu.VMEM((768, 256), bf16),
            pltpu.VMEM((768, 256), bf16),
            pltpu.VMEM((2, 48, rows, 128), f32),
            pltpu.VMEM((2, 48, rows, 128), bf16),
            pltpu.VMEM((2, 768, 128), f32),
            pltpu.VMEM((2, 768, 256), bf16),
            pltpu.VMEM((32, 256, 128), bf16),
            pltpu.VMEM((32, 256, 128), bf16),
            pltpu.VMEM((1024, 1536), bf16),
            pltpu.VMEM((6, 128, 1536), f32),
            pltpu.VMEM((2, 128, 256), bf16),
            pltpu.VMEM((2, 512, 256), bf16),
            pltpu.VMEM((1024, 128), f32),
            pltpu.VMEM((128, 1024), bf16),
            pltpu.VMEM((128, 1024), bf16),
            pltpu.VMEM((512, 128), bf16),
            pltpu.VMEM((128, 512), bf16),
            pltpu.VMEM((128, 128), f32),
            pltpu.VMEM((128, 128), f32),
            pltpu.VMEM((128, 128), f32),
            pltpu.VMEM((128, 128), f32),
            pltpu.VMEM((512, 128), f32),
            dma((2,)),
            dma((2, 2, 4)),
            dma((2, 2, 4)),
            dma((2, 4)),
            dma((2, 4)),
            dma((2, 8)),
            dma((2, 8)),
            dma((2, 2, 8)),
            dma((2, 2, 8)),
            dma((2, 6)),
            dma((2, 2, 6)),
            dma((2, 6)),
        ],
        compiler_params=pltpu.CompilerParams(
            collective_id=0, has_side_effects=True, vmem_limit_bytes=48 * 1024 * 1024
        ),
        name="fused",
    )(*args)
    return out.reshape(48, 192, 128)


def shards(
    alignment,
    alignment_norm_gain,
    alignment_norm_bias,
    projection_weight,
    projection_bias_pair,
    *rest,
):
    return fused(
        alignment,
        alignment_norm_gain,
        alignment_norm_bias,
        projection_weight.T,
        projection_bias_pair,
        *rest,
    )


def solution(mesh):
    return jax.shard_map(
        shards,
        mesh=mesh,
        in_specs=(P("row", "col", None),) + (P(),) * 12,
        out_specs=P("row", "col", None),
        check_vma=False,
    )
```

time: 107 us -> 87.2 us (0.81)
  Pallas kernels: 88 us -> 75.6 us
  local copies, waits for them, and re-layouts: 16.6 us -> 11.2 us
  other arithmetic: 1.54 us -> 0 us
    pallas_call x2 -> x1, Pallas kernels: 88 us -> 75.6 us  [fused(): pl.pallas_call(fused_kernel, in_specs=[vmem] * len(args), out_specs=vmem,...]
    broadcast_in_dim x5 -> x0, local copies, waits for them, and re-layouts: 7.05 us -> none  [pair_block(): col = lambda v: v[:, None]]
    unnamed x16 -> x27, local copies, waits for them, and re-layouts: 8.41 us -> 11.2 us
where the time goes in v3:
time: 87.2 us; the launch traced here: 86.9 us
  Pallas kernels  75.6 us (87%)
  local copies, waits for them, and re-layouts  11.2 us (13%)
    pallas_call x1, Pallas kernels, fused(): pl.pallas_call(fused_kernel, in_specs=[vmem] * len(args), out_specs=vmem,...  75.6 us
    unnamed x27, local copies, waits for them, and re-layouts  11.2 us

profile of v3, /device:TPU:12, one launch (start us, length us, event | category | flops | bytes accessed | tf_op | source)
XLA Modules:
  0.0 86.9 jit_solution(6932777393011708004)
XLA Ops:
  0.0 0.0 copy-start
  0.0 1.0 %copy-done = bf16[4,192,256]{2,1,0:T(8,128)(2,1)S(1)} copy-done((bf16[4,192,256]{2,1,0:T(8,128)(2,1)S(1)}, bf16[4,192,256]{2,1,0:T(8,128)(2,1)}, u32[]{:S(2)}) %copy-start) | copy-done | bytes 393240
  1.0 0.0 copy-start.1
  1.0 0.9 %copy-done.1 = bf16[1024,128]{1,0:T(8,128)(2,1)S(1)} copy-done((bf16[1024,128]{1,0:T(8,128)(2,1)S(1)}, bf16[1024,128]{1,0:T(8,128)(2,1)}, u32[]{:S(2)}) %copy-start.1) | copy-done | bytes 262168
  1.9 0.0 copy-start.2
  1.9 0.9 %copy-done.2 = bf16[128,512]{1,0:T(8,128)(2,1)S(1)} copy-done((bf16[128,512]{1,0:T(8,128)(2,1)S(1)}, bf16[128,512]{1,0:T(8,128)(2,1)}, u32[]{:S(2)}) %copy-start.2) | copy-done | bytes 131096
  2.9 0.0 copy-start.3
  2.9 0.9 %copy-done.3 = bf16[512,128]{1,0:T(8,128)(2,1)S(1)} copy-done((bf16[512,128]{1,0:T(8,128)(2,1)S(1)}, bf16[512,128]{1,0:T(8,128)(2,1)}, u32[]{:S(2)}) %copy-start.3) | copy-done | bytes 131096
  3.8 0.0 copy-start.4
  3.8 0.8 copy-done.4
  4.5 0.0 copy-start.5
  4.5 0.7 copy-done.5
  5.2 0.0 copy-start.6
  5.2 0.7 copy-done.6
  5.9 0.0 copy-start.7
  5.9 0.7 copy-done.7
  6.6 0.0 copy-start.8
  6.6 0.7 copy-done.8
  7.2 0.0 copy-start.9
  7.2 0.7 copy-done.9
  7.9 0.0 copy-start.10
  7.9 0.7 copy-done.10
  8.5 0.0 copy-start.11
  8.5 0.7 copy-done.11
  9.2 0.0 copy-start.12
  9.2 0.7 copy-done.12
  9.8 75.6 %fused.1 = bf16[2,24,192,128]{3,2,1,0:T(8,128)(2,1)S(1)} custom-call(bf16[4,192,256]{2,1,0:T(8,128)(2,1)S(1)} %copy-done, f32[1,256]{1,0:T(1,128)S(1)} %bitcast.13, f32[1,256]{1,0:T(1,128)S(1)} %bitcast.14, bf16[64,256]{1,0:T(8,128)(2,1)S(1)} %bitcast.11, f32[1,64]{1,0:T(1,128)S(1)} %bitcast.15, bf16[1024,128]{1,0:T(8,128)(2,1)S(1)} %copy-done.1, ...), custom_call_target="tpu_custom_call" | custom-call | tf_op jit(solution)/shard_map/fused/pallas_call | solution.py:419
  85.5 1.4 %copy.15 = bf16[48,192,128]{2,1,0:T(8,128)(2,1)} copy(bf16[48,192,128]{2,1,0:T(8,128)(2,1)S(1)} %bitcast.10) | data formatting | bytes 4718592
Async XLA Ops:
  0.0 1.0 %copy-start = (bf16[4,192,256]{2,1,0:T(8,128)(2,1)S(1)}, bf16[4,192,256]{2,1,0:T(8,128)(2,1)}, u32[]{:S(2)}) copy-start(bf16[4,192,256]{2,1,0:T(8,128)(2,1)} %x_ref.1) | copy-start | bytes 1179652
  1.0 0.9 %copy-start.1 = (bf16[1024,128]{1,0:T(8,128)(2,1)S(1)}, bf16[1024,128]{1,0:T(8,128)(2,1)}, u32[]{:S(2)}) copy-start(bf16[1024,128]{1,0:T(8,128)(2,1)} %w_out.1) | copy-start | bytes 786436
  1.9 0.9 %copy-start.2 = (bf16[128,512]{1,0:T(8,128)(2,1)S(1)}, bf16[128,512]{1,0:T(8,128)(2,1)}, u32[]{:S(2)}) copy-start(bf16[128,512]{1,0:T(8,128)(2,1)} %w_up.1) | copy-start | bytes 393220
  2.9 0.9 %copy-start.3 = (bf16[512,128]{1,0:T(8,128)(2,1)S(1)}, bf16[512,128]{1,0:T(8,128)(2,1)}, u32[]{:S(2)}) copy-start(bf16[512,128]{1,0:T(8,128)(2,1)} %w_down.1) | copy-start | bytes 393220
  3.8 0.8 copy-start.4
  4.5 0.7 copy-start.5
  5.2 0.7 copy-start.6
  5.9 0.7 copy-start.7
  6.6 0.7 copy-start.8
  7.2 0.7 copy-start.9
  7.9 0.7 copy-start.10
  8.5 0.7 copy-start.11
  9.2 0.7 copy-start.12

commit v4 on v3

--- a/solution.py
+++ b/solution.py
@@ -36,8 +36,20 @@
 
 
 def fused_kernel(
-    x_ref, gain_ref, bias_ref, w_ref, pbias_ref, w_out, bout, pg, pb, w_up, bup, w_down, bdn, out,
-    g, hl, hr, stage, block, hstage, hsend, r1f, r1m, pbuf, zbuf, nbuf, hbuf, wtmp,
+    *refs,
+):
+    ins, vins = refs[:13], refs[14:27]
+    out = refs[13]
+    in_sem = refs[27]
+    fetch = [pltpu.make_async_copy(a, v, in_sem.at[i]) for i, (a, v) in enumerate(zip(ins, vins))]
+    for c in fetch:
+        c.start()
+    fused_body(fetch, *vins, out, *refs[28:])
+
+
+def fused_body(
+    fetch, x_ref, gain_ref, bias_ref, w_ref, pbias_ref, w_out, bout, pg, pb, w_up, bup, w_down, bdn, out,
+    obuf, o_sem, g, hl, hr, stage, block, hstage, hsend, r1f, r1m, pbuf, zbuf, nbuf, hbuf, wtmp,
     wf, wm, wup, wdn, bout_b, pg_b, pb_b, bdn_b, bup_b,
     own_sem, l_send, l_recv, r_send, r_recv, y_send, y_recv, p_send, p_recv, hs_sem, hf_sem, h_recv,
 ):
@@ -79,10 +91,14 @@
     facing = (row_of(1 - ylo, z, core), (1 - yhi) * XN + x)
 
     barrier = pltpu.get_barrier_semaphore()
-    others = (up, down, across, partner, xup, xdn, facing)
+    far = (row, yhi * XN + lax.rem(x + 2, XN))
+    diagonal = [(facing[0], (1 - yhi) * XN + lax.rem(x + d, XN)) for d in range(1, XN)]
+    others = (up, down, across, partner, xup, xdn, far, facing, *diagonal)
     for dev in others:
         pl.semaphore_signal(barrier, inc=1, device_id=dev, device_id_type=MESH)
 
+    for c in fetch[:5]:
+        c.wait()
     project_block(x_ref, gain_ref, bias_ref, w_ref, pbias_ref, stage)
     block[...] = stage[...].astype(bf16)
     own = [pltpu.make_async_copy(block.at[h], g.at[h, :, row], own_sem.at[h]) for h in range(2)]
@@ -136,6 +152,8 @@
     ring_r(0)
     pslot(0, 0, ylo, 0)
     pslot(1, 0, ylo, 0)
+    for c in fetch[5:]:
+        c.wait()
     prepare_weights()
     arrived(slot(0, 1 - ylo, 0, core), y_recv.at[0, 0])
     ring_l(1, 1 - ylo, 0)
@@ -188,6 +206,13 @@
             chunk(hsend.at[h], k), chunk(dst, k), hs_sem.at[h, k], h_recv.at[h, k], device_id=facing, device_id_type=MESH
         )
 
+    def direct(h, dst, k, way):
+        step_ = (1, XN - 1, 2)[way]
+        dev = (jnp.where(ylo == yhi, row, facing[0]), jnp.where(ylo == yhi, yhi, 1 - yhi) * XN + lax.rem(x + step_, XN))
+        return pltpu.make_async_remote_copy(
+            chunk(hsend.at[h], k), chunk(dst, k), hf_sem.at[h, way, k], h_recv.at[h, k], device_id=dev, device_id_type=MESH
+        )
+
     def onward(h, dst, k, way):
         return copy(chunk(dst, k), hf_sem.at[h, way, k], h_recv.at[h, k], (xup, xdn)[way])
 
@@ -208,25 +233,35 @@
         def _():
             for k in range(6):
                 local(h, dst, k).start()
+                direct(h, dst, k, 0).start()
+                direct(h, dst, k, 1).start()
+                if k == 0:
+                    direct(h, dst, k, 2).start()
 
         @pl.when(ylo != yhi)
         def _():
             for k in range(6):
                 first(h, dst, k).start()
-
-    def onward_root(h, dst, k):
+                if k == 0:
+                    for way in range(3):
+                        direct(h, dst, k, way).start()
+
+    def pass_root(h, dst, k):
         @pl.when(offset == 0)
         def _():
             local(h, dst, k).wait()
+
+        @pl.when(far_source & (k > 0))
+        def _():
             onward(h, dst, k, 0).start()
             onward(h, dst, k, 1).start()
 
-    def onward_side(h, dst, k):
+    def pass_side(h, dst, k):
         @pl.when((offset == 1) | (offset == 3))
         def _():
             local(h, dst, k).wait()
 
-        @pl.when((offset == 1) & (lax.rem(k, 2) == 0))
+        @pl.when((offset == 1) & (lax.rem(k, 2) == 0) & (k > 0))
         def _():
             onward(h, dst, k, 0).start()
 
@@ -234,7 +269,7 @@
         def _():
             onward(h, dst, k, 1).start()
 
-    def onward_far(h, dst, k):
+    def pass_far(h, dst, k):
         @pl.when(offset == 2)
         def _():
             local(h, dst, k).wait()
@@ -261,7 +296,7 @@
         v = ref[rows, :]
         return jnp.concatenate([v, v], axis=1)
 
-    def outer_unit(k, d, bp):
+    def outer_unit(k, d, slot_, bp):
         lref, rref, half = ((hl, r1f, 1), (hr, r1m, 0))[d]
         both = lref[pl.ds(pl.multiple_of(k * 128, 128), 128), :]
         lhs0 = jnp.concatenate([both[:, 0:128], both[:, 128:256]], axis=0)
@@ -274,13 +309,13 @@
             rows = slice(b * 32, b * 32 + 32)
             lanes = slice(e * 128, e * 128 + 128)
             for i in range(8):
-                pbuf[rows, i * 128 : i * 128 + 128] = o0[i * 32 : i * 32 + 32, lanes]
+                pbuf[slot_, rows, i * 128 : i * 128 + 128] = o0[i * 32 : i * 32 + 32, lanes]
             for i in range(4):
-                pbuf[rows, (8 + i) * 128 : (9 + i) * 128] = o1[i * 32 : i * 32 + 32, lanes]
-
-    def project_chunk(k, d, n):
+                pbuf[slot_, rows, (8 + i) * 128 : (9 + i) * 128] = o1[i * 32 : i * 32 + 32, lanes]
+
+    def project_chunk(k, d, slot_, n):
         cols = slice(n * 256, n * 256 + 256)
-        z_ = jnp.dot((wf, wm)[d][...], pbuf[:, cols], preferred_element_type=f32)
+        z_ = jnp.dot((wf, wm)[d][...], pbuf[slot_, :, cols], preferred_element_type=f32)
         z_ = jnp.maximum(z_ + twice(bout_b), 0.0)
         zbuf[k, :, cols] = z_ if d == 0 else zbuf[k, :, cols] + z_
 
@@ -304,19 +339,31 @@
             t = res[:, e * 128 : e * 128 + 128].T.astype(bf16)
             for q_ in range(4):
                 if c < 8:
-                    out[c // 4, 4 * k + c % 4, 48 * q_ : 48 * q_ + 32, :] = t[32 * q_ : 32 * q_ + 32]
+                    obuf[c // 4, 4 * k + c % 4, 48 * q_ : 48 * q_ + 32, :] = t[32 * q_ : 32 * q_ + 32]
                 else:
-                    out[0, 4 * k + c - 8, 48 * q_ + 32 : 48 * q_ + 48, :] = t[16 * q_ : 16 * q_ + 16]
-                    out[1, 4 * k + c - 8, 48 * q_ + 32 : 48 * q_ + 48, :] = t[64 + 16 * q_ : 80 + 16 * q_]
+                    obuf[0, 4 * k + c - 8, 48 * q_ + 32 : 48 * q_ + 48, :] = t[16 * q_ : 16 * q_ + 16]
+                    obuf[1, 4 * k + c - 8, 48 * q_ + 32 : 48 * q_ + 48, :] = t[64 + 16 * q_ : 80 + 16 * q_]
+
+    def outer(k, d, slot_):
+        return [functools.partial(outer_unit, k, d, slot_, bp) for bp in range(16)]
+
+    def project(k, d, slot_):
+        return [functools.partial(project_chunk, k, d, slot_, n) for n in range(6)]
 
     def transition(k):
         stages = []
-        for n in range(6):
-            stages.append(functools.partial(norm_chunk, k, n))
+        for n in range(0, 6, 2):
+            both = (n, n + 1)
+            stages += [functools.partial(norm_chunk, k, m) for m in both]
             for part in range(4):
-                stages.append(functools.partial(up_chunk, n, part))
-            stages.append(functools.partial(down_chunk, k, n))
+                stages += [functools.partial(up_chunk, m, part) for m in both]
+            stages += [functools.partial(down_chunk, k, m) for m in both]
         return stages
+
+    def interleave(*lists):
+        steps = [((i + 0.5) / len(l), j, f) for j, l in enumerate(lists) for i, f in enumerate(l)]
+        for _, _, f in sorted(steps, key=lambda t: t[:2]):
+            f()
 
     partner_arrived(0)
 
@@ -325,70 +372,80 @@
         make_rows(0, hl)
 
     partner_arrived(1)
+    spread(1, r1f)
 
     @pl.when(offset == 0)
     def _():
-        onward_root(0, hl, 0)
         make_rows(1, hr)
 
-    spread(1, r1f)
     spread(0, r1m)
-    onward_side(0, hl, 0)
-    onward_far(0, hl, 0)
-
-    def left_pass(k, carry):
-        for bp in range(16):
-            outer_unit(k, 0, bp)
-
-        @pl.when(k < 5)
-        def _():
-            onward_root(0, hl, k + 1)
-            onward_side(0, hl, k + 1)
-            onward_far(0, hl, k + 1)
+
+    def pass_left(k):
+        pass_root(0, hl, k)
+        pass_side(0, hl, k)
+        pass_far(0, hl, k)
+
+    pass_left(0)
+    interleave(outer(0, 0, 0))
+
+    def left_step(k, parity):
+        pass_left(k + 1)
 
         @pl.when(k >= 1)
         def _():
-            onward_root(1, hr, k - 1)
+            pass_root(1, hr, k - 1)
 
         @pl.when(k >= 3)
         def _():
-            onward_side(1, hr, k - 3)
-
-        for n in range(6):
-            project_chunk(k, 0, n)
+            pass_side(1, hr, k - 3)
+
+        interleave(outer(k + 1, 0, 1 - parity), project(k, 0, parity))
+
+    def left_pair(t, carry):
+        left_step(2 * t, 0)
+        left_step(2 * t + 1, 1)
         return carry
 
-    lax.fori_loop(0, 6, left_pass, 0)
-
-    onward_far(1, hr, 0)
-    for bp in range(16):
-        outer_unit(0, 1, bp)
-    onward_root(1, hr, 5)
-    onward_side(1, hr, 3)
-    for n in range(6):
-        project_chunk(0, 1, n)
-
-    def right_pass(k, carry):
-        onward_far(1, hr, k)
-        stages = transition(k - 1)
-        done = 0
-        for bp in range(16):
-            outer_unit(k, 1, bp)
-            while done < (bp + 1) * len(stages) // 16:
-                stages[done]()
-                done += 1
-
+    lax.fori_loop(0, 2, left_pair, 0)
+    left_step(jnp.int32(4), 0)
+
+    pass_root(1, hr, 4)
+    pass_root(1, hr, 5)
+    pass_side(1, hr, 2)
+    pass_far(1, hr, 0)
+    interleave(outer(0, 1, 0), project(5, 0, 1))
+    pass_side(1, hr, 3)
+    pass_far(1, hr, 1)
+    interleave(outer(1, 1, 1), project(0, 1, 0))
+
+    def results(k):
+        return [
+            pltpu.make_async_copy(obuf.at[w, pl.ds(4 * k, 4)], out.at[w, pl.ds(4 * k, 4)], o_sem.at[w, k])
+            for w in range(2)
+        ]
+
+    def right_step(k, parity):
         @pl.when(k < 3)
         def _():
-            onward_side(1, hr, k + 3)
-
-        for n in range(6):
-            project_chunk(k, 1, n)
+            pass_side(1, hr, k + 3)
+
+        pass_far(1, hr, k + 1)
+        interleave(outer(k + 1, 1, 1 - parity), project(k, 1, parity), transition(k - 1))
+        for c in results(k - 1):
+            c.start()
+
+    def right_pair(t, carry):
+        right_step(2 * t + 1, 1)
+        right_step(2 * t + 2, 0)
         return carry
 
-    lax.fori_loop(1, 6, right_pass, 0)
-    for stage_ in transition(5):
-        stage_()
+    lax.fori_loop(0, 2, right_pair, 0)
+    interleave(project(5, 1, 1), transition(4))
+    for c in results(4):
+        c.start()
+    interleave(transition(5))
+    for c in results(5):
+        c.start()
 
     for h, dst in ((0, hl), (1, hr)):
         for k in range(6):
@@ -399,29 +456,36 @@
 
             @pl.when(offset == 0)
             def _(h=h, dst=dst, k=k):
-                onward(h, dst, k, 0).wait_send()
-                onward(h, dst, k, 1).wait_send()
-
-            @pl.when(offset == (1, 3)[k % 2])
-            def _(h=h, dst=dst, k=k):
-                onward(h, dst, k, k % 2).wait_send()
+                for way in range(3 if k == 0 else 2):
+                    direct(h, dst, k, way).wait_send()
+
+            if k > 0:
+
+                @pl.when(offset == (1, 3)[k % 2])
+                def _(h=h, dst=dst, k=k):
+                    onward(h, dst, k, k % 2).wait_send()
 
     for c in sent:
         c.wait_send()
+    for k in range(6):
+        for c in results(k):
+            c.wait()
 
 
 def fused(x, *params):
     rows = x.shape[0]
     bf16, f32 = jnp.bfloat16, jnp.float32
-    vmem = pl.BlockSpec(memory_space=pltpu.VMEM)
     dma = pltpu.SemaphoreType.DMA
     args = (x,) + tuple(p[None, :] if p.ndim == 1 else p for p in params)
     out = pl.pallas_call(
         fused_kernel,
-        in_specs=[vmem] * len(args),
-        out_specs=vmem,
+        in_specs=[pl.BlockSpec(memory_space=pltpu.HBM)] * len(args),
+        out_specs=pl.BlockSpec(memory_space=pltpu.HBM),
         out_shape=jax.ShapeDtypeStruct((2, 24, 192, 128), bf16),
-        scratch_shapes=[
+        scratch_shapes=[pltpu.VMEM(a.shape, a.dtype) for a in args] + [
+            dma((len(args),)),
+            pltpu.VMEM((2, 24, 192, 128), bf16),
+            dma((2, 6)),
             pltpu.VMEM((2, 48, 32, rows, 128), bf16),
             pltpu.VMEM((768, 256), bf16),
             pltpu.VMEM((768, 256), bf16),
@@ -431,7 +495,7 @@
             pltpu.VMEM((2, 768, 256), bf16),
             pltpu.VMEM((32, 256, 128), bf16),
             pltpu.VMEM((32, 256, 128), bf16),
-            pltpu.VMEM((1024, 1536), bf16),
+            pltpu.VMEM((2, 1024, 1536), bf16),
             pltpu.VMEM((6, 128, 1536), f32),
             pltpu.VMEM((2, 128, 256), bf16),
             pltpu.VMEM((2, 512, 256), bf16),
@@ -455,11 +519,11 @@
             dma((2, 2, 8)),
             dma((2, 2, 8)),
             dma((2, 6)),
-            dma((2, 2, 6)),
+            dma((2, 3, 6)),
             dma((2, 6)),
         ],
         compiler_params=pltpu.CompilerParams(
-            collective_id=0, has_side_effects=True, vmem_limit_bytes=48 * 1024 * 1024
+            collective_id=0, has_side_effects=True, vmem_limit_bytes=67043328
         ),
         name="fused",
     )(*args)

time: 87.2 us -> 76.5 us (0.88)
  local copies, waits for them, and re-layouts: 11.2 us -> 3.22 us
  Pallas kernels: 75.6 us -> 72.8 us
    unnamed x27 -> x1, local copies, waits for them, and re-layouts: 11.2 us -> 3.22 us
    pallas_call x1, Pallas kernels: 75.6 us -> 72.8 us  [fused(): pl.pallas_call(fused_kernel, in_specs=[pl.BlockSpec(memory_space=pltpu.HB...]
where the time goes in v4:
time: 76.5 us; the launch traced here: 76.1 us
  Pallas kernels  72.8 us (95%)
  local copies, waits for them, and re-layouts  3.22 us (4%)
    pallas_call x1, Pallas kernels, fused(): pl.pallas_call(fused_kernel, in_specs=[pl.BlockSpec(memory_space=pltpu.HB...  72.8 us
    unnamed x1, local copies, waits for them, and re-layouts  3.22 us

profile of v4, /device:TPU:12, one launch (start us, length us, event | category | flops | bytes accessed | tf_op | source)
XLA Modules:
  0.0 76.1 jit_solution(7887775178883529477)
XLA Ops:
  0.0 72.8 %fused.1 = bf16[2,24,192,128]{3,2,1,0:T(8,128)(2,1)} custom-call(bf16[4,192,256]{2,1,0:T(8,128)(2,1)} %refs_0_.1, f32[1,256]{1,0:T(1,128)} %bitcast.13, f32[1,256]{1,0:T(1,128)} %bitcast.14, bf16[64,256]{1,0:T(8,128)(2,1)} %bitcast.11, f32[1,64]{1,0:T(1,128)} %bitcast.15, bf16[1024,128]{1,0:T(8,128)(2,1)} %refs_5_.1, f32[1,128]{1,0:T(1,128)} %bitcast.16, ...), custom_call_target="tpu_custom_call" | custom-call | tf_op jit(solution)/shard_map/fused/pallas_call | solution.py:480
  72.8 3.2 %copy.15 = bf16[48,192,128]{2,1,0:T(8,128)(2,1)} copy(bf16[48,192,128]{2,1,0:T(8,128)(2,1)} %bitcast.10) | data formatting | bytes 4718592

commit v5 on v4

--- a/solution.py
+++ b/solution.py
@@ -49,9 +49,9 @@
 
 def fused_body(
     fetch, x_ref, gain_ref, bias_ref, w_ref, pbias_ref, w_out, bout, pg, pb, w_up, bup, w_down, bdn, out,
-    obuf, o_sem, g, hl, hr, stage, block, hstage, hsend, r1f, r1m, pbuf, zbuf, nbuf, hbuf, wtmp,
+    g, hl, hr, stage, block, hstage, hsend, r1f, r1m, pbuf, zbuf, nbuf, hbuf, wtmp,
     wf, wm, wup, wdn, bout_b, pg_b, pb_b, bdn_b, bup_b,
-    own_sem, l_send, l_recv, r_send, r_recv, y_send, y_recv, p_send, p_recv, hs_sem, hf_sem, h_recv,
+    own_sem, z_send, z_recv, y_send, y_recv, p_send, p_recv, hs_sem, hf_sem, h_recv,
 ):
     bf16, f32 = jnp.bfloat16, jnp.float32
 
@@ -93,7 +93,8 @@
     barrier = pltpu.get_barrier_semaphore()
     far = (row, yhi * XN + lax.rem(x + 2, XN))
     diagonal = [(facing[0], (1 - yhi) * XN + lax.rem(x + d, XN)) for d in range(1, XN)]
-    others = (up, down, across, partner, xup, xdn, far, facing, *diagonal)
+    near2 = [(row_of(ylo, lax.rem(z + d, ZN), core), col) for d in (2, ZN - 2)]
+    others = (up, down, *near2, across, partner, xup, xdn, far, facing, *diagonal)
     for dev in others:
         pl.semaphore_signal(barrier, inc=1, device_id=dev, device_id_type=MESH)
 
@@ -123,67 +124,84 @@
     def arrived(ref, r):
         copy(ref, own_sem.at[0], r, partner).wait_recv()
 
-    def ring_l(which, ylo_, dz):
-        top, bottom = (4, 3) if which == 0 else (3, 4)
-        ref = slot(0, ylo_, dz, core)
-        if dz <= 0 and -dz < top:
-            t = -dz
-            send(ref, l_send.at[which, 0, t], l_recv.at[which, 0, t], up)
-        if dz >= 0 and dz < bottom:
-            t = dz
-            send(ref, l_send.at[which, 1, t], l_recv.at[which, 1, t], down)
-
-    def ring_r(dz):
-        ref = slot(1, ylo, dz, core)
-        if dz <= 0 and -dz < 4:
-            send(ref, r_send.at[0, -dz], r_recv.at[0, -dz], up)
-        if dz >= 0 and dz < 3:
-            send(ref, r_send.at[1, dz], r_recv.at[1, dz], down)
-        send(ref, y_send.at[1, dz + 4], y_recv.at[1, dz + 4], across)
-
-    def pslot(h, which, ylo_, dz):
-        i = (dz + 4) % 8
-        send(slot(h, ylo_, dz, core), p_send.at[h, which, i], p_recv.at[h, which, i], partner)
+    up2 = (row_of(ylo, lax.rem(z + 2, ZN), core), col)
+    down2 = (row_of(ylo, lax.rem(z + ZN - 2, ZN), core), col)
+
+    def along(h, dz, there, dev):
+        send(slot(h, ylo, dz, core), z_send.at[h, there + 4], z_recv.at[h, there + 4], dev)
+
+    def got(h, dz):
+        arrived(slot(h, ylo, dz, core), z_recv.at[h, dz + 4])
+
+    def over(h, dz):
+        send(slot(h, ylo, dz, core), y_send.at[h, dz + 4], y_recv.at[h, dz + 4], across)
+
+    def got_over(h, dz):
+        arrived(slot(h, 1 - ylo, dz, core), y_recv.at[h, dz + 4])
+
+    def share(h, ylo_, dz):
+        copy(slot(h, ylo_, dz, core), p_send.at[h], p_recv.at[h], partner).start()
+
+    def shared(h):
+        whole = g.at[h, 0:24]
+        return copy(whole, p_send.at[h], p_recv.at[h], partner)
 
     own[0].wait()
+    along(0, 0, -1, up)
+    along(0, 0, 1, down)
+    along(0, 0, -2, up2)
+    along(0, 0, 2, down2)
+    over(0, 0)
+    share(0, ylo, 0)
     own[1].wait()
-    ring_l(0, ylo, 0)
-    send(slot(0, ylo, 0, core), y_send.at[0, 0], y_recv.at[0, 0], across)
-    ring_r(0)
-    pslot(0, 0, ylo, 0)
-    pslot(1, 0, ylo, 0)
+    along(1, 0, -1, up)
+    along(1, 0, 1, down)
+    share(1, ylo, 0)
     for c in fetch[5:]:
         c.wait()
     prepare_weights()
-    arrived(slot(0, 1 - ylo, 0, core), y_recv.at[0, 0])
-    ring_l(1, 1 - ylo, 0)
-    pslot(0, 1, 1 - ylo, 0)
-    prev = [0]
-    for t in range(1, 5):
-        for dz in (-t, t):
-            if dz == 4:
-                continue
-            way = 0 if dz < 0 else 1
-            arrived(slot(0, ylo, dz, core), l_recv.at[0, way, t - 1])
-            ring_l(0, ylo, dz)
-            arrived(slot(1, ylo, dz, core), r_recv.at[way, t - 1])
-            ring_r(dz)
-            pslot(0, 0, ylo, dz)
-            pslot(1, 0, ylo, dz)
-        for dz in (-t, t):
-            if dz == -4:
-                continue
-            way = 0 if dz < 0 else 1
-            arrived(slot(0, 1 - ylo, dz, core), l_recv.at[1, way, t - 1])
-            ring_l(1, 1 - ylo, dz)
-            pslot(0, 1, 1 - ylo, dz)
-        for dz in prev:
-            arrived(slot(1, 1 - ylo, dz, core), y_recv.at[1, dz + 4])
-            pslot(1, 1, 1 - ylo, dz)
-        prev = [dz for dz in (-t, t) if dz != 4]
-    for dz in prev:
-        arrived(slot(1, 1 - ylo, dz, core), y_recv.at[1, dz + 4])
-        pslot(1, 1, 1 - ylo, dz)
+    for dz in (-1, 1):
+        got(0, dz)
+        over(0, dz)
+        share(0, ylo, dz)
+    got(0, -2)
+    along(0, -2, -3, up)
+    along(0, -2, -4, up2)
+    over(0, -2)
+    share(0, ylo, -2)
+    got(0, 2)
+    along(0, 2, 3, down)
+    over(0, 2)
+    share(0, ylo, 2)
+    for dz in (-1, 1):
+        got(1, dz)
+        along(1, dz, dz * 2, up if dz < 0 else down)
+        share(1, ylo, dz)
+    for dz in (-3, 3, -4):
+        got(0, dz)
+        over(0, dz)
+        share(0, ylo, dz)
+    for dz in (-2, 2):
+        got(1, dz)
+        along(1, dz, dz * 3 // 2, up if dz < 0 else down)
+        share(1, ylo, dz)
+    for dz in (0, -1, 1, -2, 2):
+        got_over(0, dz)
+        share(0, 1 - ylo, dz)
+    got(1, -3)
+    along(1, -3, -4, up)
+    share(1, ylo, -3)
+    for dz in (-3, 3, -4):
+        got_over(0, dz)
+        share(0, 1 - ylo, dz)
+    for dz in (0, -1, 1, -2, 2, -3):
+        over(1, dz)
+    got(1, 3)
+    over(1, 3)
+    share(1, ylo, 3)
+    got(1, -4)
+    over(1, -4)
+    share(1, ylo, -4)
 
     offset = lax.rem(x - z // 2 + XN, XN)
     q = lax.rem(row, 4)
@@ -216,7 +234,7 @@
     def onward(h, dst, k, way):
         return copy(chunk(dst, k), hf_sem.at[h, way, k], h_recv.at[h, k], (xup, xdn)[way])
 
-    def make_rows(h, dst):
+    def make_rows(h):
         for p in range(16):
             a0 = pltpu.roll(flat[h, p].astype(f32), shift0, axis=1)
             a1 = pltpu.roll(flat[h, p + 16].astype(f32), shift1, axis=1)
@@ -229,29 +247,29 @@
         hsend[h, :, 0:128] = hstage[0].astype(bf16)
         hsend[h, :, 128:256] = hstage[1].astype(bf16)
 
-        @pl.when(ylo == yhi)
-        def _():
-            for k in range(6):
-                local(h, dst, k).start()
-                direct(h, dst, k, 0).start()
-                direct(h, dst, k, 1).start()
-                if k == 0:
-                    direct(h, dst, k, 2).start()
-
-        @pl.when(ylo != yhi)
-        def _():
-            for k in range(6):
-                first(h, dst, k).start()
-                if k == 0:
-                    for way in range(3):
-                        direct(h, dst, k, way).start()
+    def send_rows(h, dst, k):
+        @pl.when(self_source)
+        def _():
+            local(h, dst, k).start()
+            direct(h, dst, k, 0).start()
+            direct(h, dst, k, 1).start()
+
+        @pl.when(far_source)
+        def _():
+            first(h, dst, k).start()
+
+        if h == 0 and isinstance(k, int):
+
+            @pl.when(offset == 0)
+            def _():
+                direct(h, dst, k, 2).start()
 
     def pass_root(h, dst, k):
         @pl.when(offset == 0)
         def _():
             local(h, dst, k).wait()
 
-        @pl.when(far_source & (k > 0))
+        @pl.when(far_source)
         def _():
             onward(h, dst, k, 0).start()
             onward(h, dst, k, 1).start()
@@ -261,7 +279,7 @@
         def _():
             local(h, dst, k).wait()
 
-        @pl.when((offset == 1) & (lax.rem(k, 2) == 0) & (k > 0))
+        @pl.when((offset == 1) & (lax.rem(k, 2) == 0) & ((k > 0) | (h > 0)))
         def _():
             onward(h, dst, k, 0).start()
 
@@ -273,12 +291,6 @@
         @pl.when(offset == 2)
         def _():
             local(h, dst, k).wait()
-
-    def partner_arrived(h):
-        for which in range(2):
-            for dz in range(-4, 4):
-                at = dz if which == 0 or dz > -4 else 4
-                arrived(slot(h, (ylo, 1 - ylo)[which], at, 1 - core), p_recv.at[h, which, (at + 4) % 8])
 
     low = lane < 64
     zero = jnp.zeros((128, 128), f32)
@@ -339,10 +351,10 @@
             t = res[:, e * 128 : e * 128 + 128].T.astype(bf16)
             for q_ in range(4):
                 if c < 8:
-                    obuf[c // 4, 4 * k + c % 4, 48 * q_ : 48 * q_ + 32, :] = t[32 * q_ : 32 * q_ + 32]
+                    out[c // 4, 4 * k + c % 4, 48 * q_ : 48 * q_ + 32, :] = t[32 * q_ : 32 * q_ + 32]
                 else:
-                    obuf[0, 4 * k + c - 8, 48 * q_ + 32 : 48 * q_ + 48, :] = t[16 * q_ : 16 * q_ + 16]
-                    obuf[1, 4 * k + c - 8, 48 * q_ + 32 : 48 * q_ + 48, :] = t[64 + 16 * q_ : 80 + 16 * q_]
+                    out[0, 4 * k + c - 8, 48 * q_ + 32 : 48 * q_ + 48, :] = t[16 * q_ : 16 * q_ + 16]
+                    out[1, 4 * k + c - 8, 48 * q_ + 32 : 48 * q_ + 48, :] = t[64 + 16 * q_ : 80 + 16 * q_]
 
     def outer(k, d, slot_):
         return [functools.partial(outer_unit, k, d, slot_, bp) for bp in range(16)]
@@ -365,74 +377,100 @@
         for _, _, f in sorted(steps, key=lambda t: t[:2]):
             f()
 
-    partner_arrived(0)
+    shared(0).wait_recv()
 
     @pl.when(offset == 0)
     def _():
-        make_rows(0, hl)
-
-    partner_arrived(1)
+        make_rows(0)
+        send_rows(0, hl, 0)
+
+    for dz in (0, -1, 1, -2, 2, -3):
+        got_over(1, dz)
+        share(1, 1 - ylo, dz)
+    spread(0, r1m)
+    for dz in (3, -4):
+        got_over(1, dz)
+        share(1, 1 - ylo, dz)
+    pass_root(0, hl, 0)
+    shared(1).wait_recv()
     spread(1, r1f)
 
     @pl.when(offset == 0)
     def _():
-        make_rows(1, hr)
-
-    spread(0, r1m)
-
-    def pass_left(k):
+        make_rows(1)
+
+    def send_left(k):
+        @pl.when(offset == 0)
+        def _():
+            send_rows(0, hl, k)
+
+    def send_right(k):
+        @pl.when(offset == 0)
+        def _():
+            send_rows(1, hr, k)
+
+    pass_side(0, hl, 0)
+    pass_far(0, hl, 0)
+    send_left(jnp.int32(1))
+    interleave(outer(0, 0, 0))
+
+    def left_step(k, parity):
         pass_root(0, hl, k)
         pass_side(0, hl, k)
         pass_far(0, hl, k)
 
-    pass_left(0)
-    interleave(outer(0, 0, 0))
-
-    def left_step(k, parity):
-        pass_left(k + 1)
-
-        @pl.when(k >= 1)
-        def _():
-            pass_root(1, hr, k - 1)
-
-        @pl.when(k >= 3)
-        def _():
-            pass_side(1, hr, k - 3)
-
-        interleave(outer(k + 1, 0, 1 - parity), project(k, 0, parity))
+        @pl.when(k < 5)
+        def _():
+            send_left(k + 1)
+
+        if parity == 1:
+            send_right((k - 1) // 2)
+
+            @pl.when(k >= 3)
+            def _():
+                pass_root(1, hr, (k - 3) // 2)
+
+            @pl.when(k >= 5)
+            def _():
+                pass_side(1, hr, (k - 5) // 2)
+
+        interleave(outer(k, 0, parity), project(k - 1, 0, 1 - parity))
 
     def left_pair(t, carry):
-        left_step(2 * t, 0)
         left_step(2 * t + 1, 1)
+        left_step(2 * t + 2, 0)
         return carry
 
     lax.fori_loop(0, 2, left_pair, 0)
-    left_step(jnp.int32(4), 0)
-
-    pass_root(1, hr, 4)
-    pass_root(1, hr, 5)
-    pass_side(1, hr, 2)
-    pass_far(1, hr, 0)
+    left_step(jnp.int32(5), 1)
+
+    one = jnp.int32(1)
+    send_right(3 * one)
+    pass_root(1, hr, 2 * one)
+    pass_side(1, hr, one)
+    pass_far(1, hr, 0 * one)
     interleave(outer(0, 1, 0), project(5, 0, 1))
-    pass_side(1, hr, 3)
-    pass_far(1, hr, 1)
+    send_right(4 * one)
+    pass_root(1, hr, 3 * one)
+    pass_side(1, hr, 2 * one)
+    pass_far(1, hr, one)
     interleave(outer(1, 1, 1), project(0, 1, 0))
 
-    def results(k):
-        return [
-            pltpu.make_async_copy(obuf.at[w, pl.ds(4 * k, 4)], out.at[w, pl.ds(4 * k, 4)], o_sem.at[w, k])
-            for w in range(2)
-        ]
-
     def right_step(k, parity):
+        @pl.when(k == 1)
+        def _():
+            send_right(5 * one)
+
         @pl.when(k < 3)
         def _():
-            pass_side(1, hr, k + 3)
+            pass_root(1, hr, k + 3)
+
+        @pl.when(k < 4)
+        def _():
+            pass_side(1, hr, k + 2)
 
         pass_far(1, hr, k + 1)
         interleave(outer(k + 1, 1, 1 - parity), project(k, 1, parity), transition(k - 1))
-        for c in results(k - 1):
-            c.start()
 
     def right_pair(t, carry):
         right_step(2 * t + 1, 1)
@@ -441,11 +479,7 @@
 
     lax.fori_loop(0, 2, right_pair, 0)
     interleave(project(5, 1, 1), transition(4))
-    for c in results(4):
-        c.start()
     interleave(transition(5))
-    for c in results(5):
-        c.start()
 
     for h, dst in ((0, hl), (1, hr)):
         for k in range(6):
@@ -456,20 +490,19 @@
 
             @pl.when(offset == 0)
             def _(h=h, dst=dst, k=k):
-                for way in range(3 if k == 0 else 2):
+                for way in range(3 if k + h == 0 else 2):
                     direct(h, dst, k, way).wait_send()
 
-            if k > 0:
+            if k + h > 0:
 
                 @pl.when(offset == (1, 3)[k % 2])
                 def _(h=h, dst=dst, k=k):
                     onward(h, dst, k, k % 2).wait_send()
 
+    for h in range(2):
+        shared(h).wait_send()
     for c in sent:
         c.wait_send()
-    for k in range(6):
-        for c in results(k):
-            c.wait()
 
 
 def fused(x, *params):
@@ -477,15 +510,15 @@
     bf16, f32 = jnp.bfloat16, jnp.float32
     dma = pltpu.SemaphoreType.DMA
     args = (x,) + tuple(p[None, :] if p.ndim == 1 else p for p in params)
+    args = tuple(pltpu.with_memory_space_constraint(a, pltpu.HBM) for a in args)
+    out_bytes = 2 * 24 * 192 * 128 * 2
     out = pl.pallas_call(
         fused_kernel,
         in_specs=[pl.BlockSpec(memory_space=pltpu.HBM)] * len(args),
-        out_specs=pl.BlockSpec(memory_space=pltpu.HBM),
+        out_specs=pl.BlockSpec(memory_space=pltpu.VMEM),
         out_shape=jax.ShapeDtypeStruct((2, 24, 192, 128), bf16),
         scratch_shapes=[pltpu.VMEM(a.shape, a.dtype) for a in args] + [
             dma((len(args),)),
-            pltpu.VMEM((2, 24, 192, 128), bf16),
-            dma((2, 6)),
             pltpu.VMEM((2, 48, 32, rows, 128), bf16),
             pltpu.VMEM((768, 256), bf16),
             pltpu.VMEM((768, 256), bf16),
@@ -510,20 +543,18 @@
             pltpu.VMEM((128, 128), f32),
             pltpu.VMEM((512, 128), f32),
             dma((2,)),
-            dma((2, 2, 4)),
-            dma((2, 2, 4)),
-            dma((2, 4)),
-            dma((2, 4)),
             dma((2, 8)),
             dma((2, 8)),
-            dma((2, 2, 8)),
-            dma((2, 2, 8)),
+            dma((2, 8)),
+            dma((2, 8)),
+            dma((2,)),
+            dma((2,)),
             dma((2, 6)),
             dma((2, 3, 6)),
             dma((2, 6)),
         ],
         compiler_params=pltpu.CompilerParams(
-            collective_id=0, has_side_effects=True, vmem_limit_bytes=67043328
+            collective_id=0, has_side_effects=True, vmem_limit_bytes=48 * 1024 * 1024
         ),
         name="fused",
     )(*args)

time: 76.5 us -> 76.8 us (level); the launches traced: 76.1 us -> 75.4 us
  local copies, waits for them, and re-layouts: 3.22 us -> 1.41 us
  Pallas kernels: 72.8 us -> 74 us
    unnamed x1, local copies, waits for them, and re-layouts: 3.22 us -> 1.41 us
    pallas_call x1, Pallas kernels: 72.8 us -> 74 us  [fused(): pl.pallas_call(fused_kernel, in_specs=[pl.BlockSpec(memory_space=pltpu.HB...]
where the time goes in v5:
time: 76.8 us; the launch traced here: 75.4 us
  Pallas kernels  74 us (96%)
  local copies, waits for them, and re-layouts  1.41 us (2%)
    pallas_call x1, Pallas kernels, fused(): pl.pallas_call(fused_kernel, in_specs=[pl.BlockSpec(memory_space=pltpu.HB...  74 us

profile of v5, /device:TPU:12, one launch (start us, length us, event | category | flops | bytes accessed | tf_op | source)
XLA Modules:
  0.0 75.4 jit_solution(664072636665531207)
XLA Ops:
  0.0 74.0 %fused.1 = bf16[2,24,192,128]{3,2,1,0:T(8,128)(2,1)S(1)} custom-call(bf16[4,192,256]{2,1,0:T(8,128)(2,1)} %refs_0_.1, f32[1,256]{1,0:T(1,128)} %bitcast.13, f32[1,256]{1,0:T(1,128)} %bitcast.14, bf16[64,256]{1,0:T(8,128)(2,1)} %bitcast.11, f32[1,64]{1,0:T(1,128)} %bitcast.15, bf16[1024,128]{1,0:T(8,128)(2,1)} %refs_5_.1, f32[1,128]{1,0:T(1,128)} %bitcast.16, ...), custom_call_target="tpu_custom_call" | custom-call | tf_op jit(solution)/shard_map/fused/pallas_call | solution.py:515
  74.0 1.4 %copy.15 = bf16[48,192,128]{2,1,0:T(8,128)(2,1)} copy(bf16[48,192,128]{2,1,0:T(8,128)(2,1)S(1)} %bitcast.10) | data formatting | bytes 4718592

commit v6 on v5

--- a/solution.py
+++ b/solution.py
@@ -51,7 +51,7 @@
     fetch, x_ref, gain_ref, bias_ref, w_ref, pbias_ref, w_out, bout, pg, pb, w_up, bup, w_down, bdn, out,
     g, hl, hr, stage, block, hstage, hsend, r1f, r1m, pbuf, zbuf, nbuf, hbuf, wtmp,
     wf, wm, wup, wdn, bout_b, pg_b, pb_b, bdn_b, bup_b,
-    own_sem, z_send, z_recv, y_send, y_recv, p_send, p_recv, hs_sem, hf_sem, h_recv,
+    own_sem, f_send, f_recv, z_send, z_recv, y_send, y_recv, p_send, p_recv, hs_sem, hf_sem, h_recv,
 ):
     bf16, f32 = jnp.bfloat16, jnp.float32
 
@@ -146,36 +146,47 @@
         whole = g.at[h, 0:24]
         return copy(whole, p_send.at[h], p_recv.at[h], partner)
 
+    def along_facing(there, dev):
+        send(slot(0, 1 - ylo, 0, core), f_send.at[there + 4], f_recv.at[there + 4], dev)
+
+    def got_facing(dz):
+        arrived(slot(0, 1 - ylo, dz, core), f_recv.at[dz + 4])
+
     own[0].wait()
+    over(0, 0)
     along(0, 0, -1, up)
     along(0, 0, 1, down)
     along(0, 0, -2, up2)
     along(0, 0, 2, down2)
-    over(0, 0)
     share(0, ylo, 0)
     own[1].wait()
     along(1, 0, -1, up)
     along(1, 0, 1, down)
+    over(1, 0)
     share(1, ylo, 0)
     for c in fetch[5:]:
         c.wait()
     prepare_weights()
+    got_over(0, 0)
+    along_facing(-1, up)
+    along_facing(1, down)
+    along_facing(-2, up2)
+    along_facing(2, down2)
+    share(0, 1 - ylo, 0)
     for dz in (-1, 1):
         got(0, dz)
-        over(0, dz)
         share(0, ylo, dz)
     got(0, -2)
     along(0, -2, -3, up)
     along(0, -2, -4, up2)
-    over(0, -2)
     share(0, ylo, -2)
     got(0, 2)
     along(0, 2, 3, down)
-    over(0, 2)
     share(0, ylo, 2)
     for dz in (-1, 1):
         got(1, dz)
         along(1, dz, dz * 2, up if dz < 0 else down)
+        over(1, dz)
         share(1, ylo, dz)
     for dz in (-3, 3, -4):
         got(0, dz)
@@ -184,24 +195,27 @@
     for dz in (-2, 2):
         got(1, dz)
         along(1, dz, dz * 3 // 2, up if dz < 0 else down)
+        over(1, dz)
         share(1, ylo, dz)
-    for dz in (0, -1, 1, -2, 2):
-        got_over(0, dz)
+    for dz in (-1, 1, -2, 2):
+        got_facing(dz)
         share(0, 1 - ylo, dz)
     got(1, -3)
     along(1, -3, -4, up)
+    over(1, -3)
     share(1, ylo, -3)
+    got(1, 3)
+    over(1, 3)
+    share(1, ylo, 3)
     for dz in (-3, 3, -4):
         got_over(0, dz)
         share(0, 1 - ylo, dz)
-    for dz in (0, -1, 1, -2, 2, -3):
-        over(1, dz)
-    got(1, 3)
-    over(1, 3)
-    share(1, ylo, 3)
     got(1, -4)
     over(1, -4)
     share(1, ylo, -4)
+    for dz in (0, -1, 1):
+        got_over(1, dz)
+        share(1, 1 - ylo, dz)
 
     offset = lax.rem(x - z // 2 + XN, XN)
     q = lax.rem(row, 4)
@@ -377,6 +391,7 @@
         for _, _, f in sorted(steps, key=lambda t: t[:2]):
             f()
 
+    one = jnp.int32(1)
     shared(0).wait_recv()
 
     @pl.when(offset == 0)
@@ -384,11 +399,16 @@
         make_rows(0)
         send_rows(0, hl, 0)
 
-    for dz in (0, -1, 1, -2, 2, -3):
+    for dz in (-2, 2):
         got_over(1, dz)
         share(1, 1 - ylo, dz)
     spread(0, r1m)
-    for dz in (3, -4):
+
+    @pl.when(offset == 0)
+    def _():
+        send_rows(0, hl, one)
+
+    for dz in (-3, 3, -4):
         got_over(1, dz)
         share(1, 1 - ylo, dz)
     pass_root(0, hl, 0)
@@ -397,6 +417,7 @@
 
     @pl.when(offset == 0)
     def _():
+        send_rows(0, hl, 2 * one)
         make_rows(1)
 
     def send_left(k):
@@ -411,7 +432,7 @@
 
     pass_side(0, hl, 0)
     pass_far(0, hl, 0)
-    send_left(jnp.int32(1))
+    send_left(3 * one)
     interleave(outer(0, 0, 0))
 
     def left_step(k, parity):
@@ -419,20 +440,19 @@
         pass_side(0, hl, k)
         pass_far(0, hl, k)
 
-        @pl.when(k < 5)
-        def _():
-            send_left(k + 1)
-
-        if parity == 1:
-            send_right((k - 1) // 2)
-
-            @pl.when(k >= 3)
-            def _():
-                pass_root(1, hr, (k - 3) // 2)
-
-            @pl.when(k >= 5)
-            def _():
-                pass_side(1, hr, (k - 5) // 2)
+        @pl.when(k < 3)
+        def _():
+            send_left(k + 3)
+
+        send_right(k - 1)
+
+        @pl.when(k >= 3)
+        def _():
+            pass_root(1, hr, k - 3)
+
+        @pl.when(k >= 5)
+        def _():
+            pass_side(1, hr, k - 5)
 
         interleave(outer(k, 0, parity), project(k - 1, 0, 1 - parity))
 
@@ -444,14 +464,12 @@
     lax.fori_loop(0, 2, left_pair, 0)
     left_step(jnp.int32(5), 1)
 
-    one = jnp.int32(1)
-    send_right(3 * one)
-    pass_root(1, hr, 2 * one)
+    send_right(5 * one)
+    pass_root(1, hr, 3 * one)
     pass_side(1, hr, one)
     pass_far(1, hr, 0 * one)
     interleave(outer(0, 1, 0), project(5, 0, 1))
-    send_right(4 * one)
-    pass_root(1, hr, 3 * one)
+    pass_root(1, hr, 4 * one)
     pass_side(1, hr, 2 * one)
     pass_far(1, hr, one)
     interleave(outer(1, 1, 1), project(0, 1, 0))
@@ -459,11 +477,7 @@
     def right_step(k, parity):
         @pl.when(k == 1)
         def _():
-            send_right(5 * one)
-
-        @pl.when(k < 3)
-        def _():
-            pass_root(1, hr, k + 3)
+            pass_root(1, hr, k + 4)
 
         @pl.when(k < 4)
         def _():
@@ -543,6 +557,8 @@
             pltpu.VMEM((128, 128), f32),
             pltpu.VMEM((512, 128), f32),
             dma((2,)),
+            dma((8,)),
+            dma((8,)),
             dma((2, 8)),
             dma((2, 8)),
             dma((2, 8)),

time: 76.8 us -> 72 us (0.938); the launches traced: 75.4 us -> 71.9 us
  Pallas kernels: 74 us -> 70.5 us
    pallas_call x1, Pallas kernels: 74 us -> 70.5 us  [fused(): pl.pallas_call(fused_kernel, in_specs=[pl.BlockSpec(memory_space=pltpu.HB...]
where the time goes in v6:
time: 72 us; the launch traced here: 71.9 us
  Pallas kernels  70.5 us (98%)
  local copies, waits for them, and re-layouts  1.41 us (2%)
    pallas_call x1, Pallas kernels, fused(): pl.pallas_call(fused_kernel, in_specs=[pl.BlockSpec(memory_space=pltpu.HB...  70.5 us

profile of v6, /device:TPU:12, one launch (start us, length us, event | category | flops | bytes accessed | tf_op | source)
XLA Modules:
  0.0 71.9 jit_solution(8853928575269987544)
XLA Ops:
  0.0 70.5 %fused.1 = bf16[2,24,192,128]{3,2,1,0:T(8,128)(2,1)S(1)} custom-call(bf16[4,192,256]{2,1,0:T(8,128)(2,1)} %refs_0_.1, f32[1,256]{1,0:T(1,128)} %bitcast.13, f32[1,256]{1,0:T(1,128)} %bitcast.14, bf16[64,256]{1,0:T(8,128)(2,1)} %bitcast.11, f32[1,64]{1,0:T(1,128)} %bitcast.15, bf16[1024,128]{1,0:T(8,128)(2,1)} %refs_5_.1, f32[1,128]{1,0:T(1,128)} %bitcast.16, ...), custom_call_target="tpu_custom_call" | custom-call | tf_op jit(solution)/shard_map/fused/pallas_call | solution.py:529
  70.5 1.4 %copy.15 = bf16[48,192,128]{2,1,0:T(8,128)(2,1)} copy(bf16[48,192,128]{2,1,0:T(8,128)(2,1)S(1)} %bitcast.10) | data formatting | bytes 4718592

commit v7 on v5

--- a/solution.py
+++ b/solution.py
@@ -51,7 +51,7 @@
     fetch, x_ref, gain_ref, bias_ref, w_ref, pbias_ref, w_out, bout, pg, pb, w_up, bup, w_down, bdn, out,
     g, hl, hr, stage, block, hstage, hsend, r1f, r1m, pbuf, zbuf, nbuf, hbuf, wtmp,
     wf, wm, wup, wdn, bout_b, pg_b, pb_b, bdn_b, bup_b,
-    own_sem, z_send, z_recv, y_send, y_recv, p_send, p_recv, hs_sem, hf_sem, h_recv,
+    own_sem, f_send, f_recv, z_send, z_recv, y_send, y_recv, p_send, p_recv, hs_sem, hf_sem, h_recv,
 ):
     bf16, f32 = jnp.bfloat16, jnp.float32
 
@@ -377,21 +377,29 @@
         for _, _, f in sorted(steps, key=lambda t: t[:2]):
             f()
 
+    one = jnp.int32(1)
     shared(0).wait_recv()
 
     @pl.when(offset == 0)
     def _():
         make_rows(0)
         send_rows(0, hl, 0)
-
-    for dz in (0, -1, 1, -2, 2, -3):
+        send_rows(0, hl, one)
+
+    for dz in (0, -1, 1, -2, 2):
         got_over(1, dz)
         share(1, 1 - ylo, dz)
     spread(0, r1m)
-    for dz in (3, -4):
+
+    @pl.when(offset == 0)
+    def _():
+        send_rows(0, hl, 2 * one)
+
+    for dz in (-3, 3, -4):
         got_over(1, dz)
         share(1, 1 - ylo, dz)
     pass_root(0, hl, 0)
+    pass_root(0, hl, one)
     shared(1).wait_recv()
     spread(1, r1f)
 
@@ -410,29 +418,33 @@
             send_rows(1, hr, k)
 
     pass_side(0, hl, 0)
+    pass_side(0, hl, one)
     pass_far(0, hl, 0)
-    send_left(jnp.int32(1))
+    send_left(3 * one)
+    send_right(0 * one)
     interleave(outer(0, 0, 0))
 
     def left_step(k, parity):
-        pass_root(0, hl, k)
-        pass_side(0, hl, k)
+        @pl.when(k < 5)
+        def _():
+            pass_root(0, hl, k + 1)
+            pass_side(0, hl, k + 1)
+
         pass_far(0, hl, k)
 
-        @pl.when(k < 5)
-        def _():
-            send_left(k + 1)
-
-        if parity == 1:
-            send_right((k - 1) // 2)
-
-            @pl.when(k >= 3)
-            def _():
-                pass_root(1, hr, (k - 3) // 2)
-
-            @pl.when(k >= 5)
-            def _():
-                pass_side(1, hr, (k - 5) // 2)
+        @pl.when(k < 3)
+        def _():
+            send_left(k + 3)
+
+        send_right(k)
+
+        @pl.when(k >= 2)
+        def _():
+            pass_root(1, hr, k - 2)
+
+        @pl.when(k >= 4)
+        def _():
+            pass_side(1, hr, k - 4)
 
         interleave(outer(k, 0, parity), project(k - 1, 0, 1 - parity))
 
@@ -444,30 +456,19 @@
     lax.fori_loop(0, 2, left_pair, 0)
     left_step(jnp.int32(5), 1)
 
-    one = jnp.int32(1)
-    send_right(3 * one)
-    pass_root(1, hr, 2 * one)
-    pass_side(1, hr, one)
+    pass_root(1, hr, 4 * one)
+    pass_side(1, hr, 2 * one)
     pass_far(1, hr, 0 * one)
     interleave(outer(0, 1, 0), project(5, 0, 1))
-    send_right(4 * one)
-    pass_root(1, hr, 3 * one)
-    pass_side(1, hr, 2 * one)
+    pass_root(1, hr, 5 * one)
+    pass_side(1, hr, 3 * one)
     pass_far(1, hr, one)
     interleave(outer(1, 1, 1), project(0, 1, 0))
 
     def right_step(k, parity):
-        @pl.when(k == 1)
-        def _():
-            send_right(5 * one)
-
         @pl.when(k < 3)
         def _():
-            pass_root(1, hr, k + 3)
-
-        @pl.when(k < 4)
-        def _():
-            pass_side(1, hr, k + 2)
+            pass_side(1, hr, k + 3)
 
         pass_far(1, hr, k + 1)
         interleave(outer(k + 1, 1, 1 - parity), project(k, 1, parity), transition(k - 1))
@@ -543,6 +544,8 @@
             pltpu.VMEM((128, 128), f32),
             pltpu.VMEM((512, 128), f32),
             dma((2,)),
+            dma((8,)),
+            dma((8,)),
             dma((2, 8)),
             dma((2, 8)),
             dma((2, 8)),

time: 76.8 us -> 68.6 us (0.89); the launches traced: 75.4 us -> 68.5 us
  Pallas kernels: 74 us -> 67.1 us
    pallas_call x1, Pallas kernels: 74 us -> 67.1 us  [fused(): pl.pallas_call(fused_kernel, in_specs=[pl.BlockSpec(memory_space=pltpu.HB...]
where the time goes in v7:
time: 68.6 us; the launch traced here: 68.5 us
  Pallas kernels  67.1 us (98%)
  local copies, waits for them, and re-layouts  1.41 us (2%)
    pallas_call x1, Pallas kernels, fused(): pl.pallas_call(fused_kernel, in_specs=[pl.BlockSpec(memory_space=pltpu.HB...  67.1 us
    unnamed x1, local copies, waits for them, and re-layouts  1.41 us

profile of v7, /device:TPU:12, one launch (start us, length us, event | category | flops | bytes accessed | tf_op | source)
XLA Modules:
  0.0 68.5 jit_solution(7464588524127737418)
XLA Ops:
  0.0 67.1 %fused.1 = bf16[2,24,192,128]{3,2,1,0:T(8,128)(2,1)S(1)} custom-call(bf16[4,192,256]{2,1,0:T(8,128)(2,1)} %refs_0_.1, f32[1,256]{1,0:T(1,128)} %bitcast.13, f32[1,256]{1,0:T(1,128)} %bitcast.14, bf16[64,256]{1,0:T(8,128)(2,1)} %bitcast.11, f32[1,64]{1,0:T(1,128)} %bitcast.15, bf16[1024,128]{1,0:T(8,128)(2,1)} %refs_5_.1, f32[1,128]{1,0:T(1,128)} %bitcast.16, ...), custom_call_target="tpu_custom_call" | custom-call | tf_op jit(solution)/shard_map/fused/pallas_call | solution.py:516
  67.1 1.4 %copy.15 = bf16[48,192,128]{2,1,0:T(8,128)(2,1)} copy(bf16[48,192,128]{2,1,0:T(8,128)(2,1)S(1)} %bitcast.10) | data formatting | bytes 4718592

commit v8 on v7

--- a/solution.py
+++ b/solution.py
@@ -181,21 +181,23 @@
         got(0, dz)
         over(0, dz)
         share(0, ylo, dz)
+    for dz in (0, -1, 1):
+        over(1, dz)
     for dz in (-2, 2):
         got(1, dz)
         along(1, dz, dz * 3 // 2, up if dz < 0 else down)
+        over(1, dz)
         share(1, ylo, dz)
     for dz in (0, -1, 1, -2, 2):
         got_over(0, dz)
         share(0, 1 - ylo, dz)
     got(1, -3)
     along(1, -3, -4, up)
+    over(1, -3)
     share(1, ylo, -3)
     for dz in (-3, 3, -4):
         got_over(0, dz)
         share(0, 1 - ylo, dz)
-    for dz in (0, -1, 1, -2, 2, -3):
-        over(1, dz)
     got(1, 3)
     over(1, 3)
     share(1, ylo, 3)
@@ -395,10 +397,10 @@
     def _():
         send_rows(0, hl, 2 * one)
 
+    pass_root(0, hl, 0)
     for dz in (-3, 3, -4):
         got_over(1, dz)
         share(1, 1 - ylo, dz)
-    pass_root(0, hl, 0)
     pass_root(0, hl, one)
     shared(1).wait_recv()
     spread(1, r1f)

time: 68.6 us -> 68.9 us (level)
  no operation moved by 1% of the time
where the time goes in v8:
time: 68.9 us; the launch traced here: 68.8 us
  Pallas kernels  67.4 us (98%)
  local copies, waits for them, and re-layouts  1.41 us (2%)
    pallas_call x1, Pallas kernels, fused(): pl.pallas_call(fused_kernel, in_specs=[pl.BlockSpec(memory_space=pltpu.HB...  67.4 us
    unnamed x1, local copies, waits for them, and re-layouts  1.41 us

profile of v8, /device:TPU:12, one launch (start us, length us, event | category | flops | bytes accessed | tf_op | source)
XLA Modules:
  0.0 68.8 jit_solution(2448461607234597217)
XLA Ops:
  0.0 67.4 %fused.1 = bf16[2,24,192,128]{3,2,1,0:T(8,128)(2,1)S(1)} custom-call(bf16[4,192,256]{2,1,0:T(8,128)(2,1)} %refs_0_.1, f32[1,256]{1,0:T(1,128)} %bitcast.13, f32[1,256]{1,0:T(1,128)} %bitcast.14, bf16[64,256]{1,0:T(8,128)(2,1)} %bitcast.11, f32[1,64]{1,0:T(1,128)} %bitcast.15, bf16[1024,128]{1,0:T(8,128)(2,1)} %refs_5_.1, f32[1,128]{1,0:T(1,128)} %bitcast.16, ...), custom_call_target="tpu_custom_call" | custom-call | tf_op jit(solution)/shard_map/fused/pallas_call | solution.py:518
  67.4 1.4 %copy.15 = bf16[48,192,128]{2,1,0:T(8,128)(2,1)} copy(bf16[48,192,128]{2,1,0:T(8,128)(2,1)S(1)} %bitcast.10) | data formatting | bytes 4718592
